TPU v7x, 256 devices: a whole 4x4x8 slice. The times are simulated.
256 devices in a mesh: phi: 16 (over z, core), gz: 16 (over y, x).
Axes of the slice: x: 4, y: 4, z: 8, core: 2. Of those that a mesh axis runs over, the one named last changes fastest.
Arguments:
- charge: float32 [1024, 256, 256], P('phi', 'gz'), may hold values from -24 to 24
- outer_held: int32 [256], replicated, may hold values 0 or 1
- end_held: int32 [256], replicated, may hold values 0 or 1
Outputs:
- potential: float32 [1024, 256, 256], P('phi', 'gz')
- scales: float32 [2, 1024], P(None, 'phi')
Inputs may be any that keep to these rules, and one draw needn't show every extreme that they name: `outer_held`: 1 holds the boundary at zero potential, 0 leaves it without flux. `end_held`: 1 holds both z ends of the radial cell at zero potential, 0 leaves them without flux.
All inputs are finite; a program needn't handle non-finite values.
Results may differ from a plain program's by a relative error of at most 0.0003.
Values sent between devices are 32-bit elements; how exact they have to be, the bound alone decides.
A program may use at most 128 MiB of HBM per device.

v0:
```python
import math

import jax
import jax.numpy as jnp
from jax import lax
from jax.sharding import PartitionSpec as P

NPHI = 1024
VCYC = 2
NU = 2
KC = 3
RIN = 131


relaxation = 0.8
small_floor = 1e-06


def hartley_table(length):
    row_ids = lax.broadcasted_iota(jnp.int32, (length, length), 0)
    col_ids = lax.broadcasted_iota(jnp.int32, (length, length), 1)
    phases = (row_ids * col_ids % length).astype(jnp.float32) * (2.0 * math.pi / length)
    return (jnp.cos(phases) + jnp.sin(phases)) * (1.0 / math.sqrt(length))


def transform_rows(hartley, values):
    flat = values.reshape(values.shape[0], -1)
    result = jnp.dot(
        hartley, flat, precision=lax.Precision.HIGHEST, preferred_element_type=jnp.float32
    )
    return result.reshape(values.shape)


def radial_terms(radial_count, coarse):
    position = jnp.arange(radial_count, dtype=jnp.float32)
    if coarse:
        radius = RIN + 2.0 * position + 1.0
        return (radius, (radius - 1.0) / (4.0 * radius), (radius + 1.0) / (4.0 * radius), 0.25)
    radius = RIN + position + 0.5
    return (radius, (radius - 0.5) / radius, (radius + 0.5) / radius, 1.0)


def diagonal(mode_ids, axial_ids, total_axial, radial, outer_bc, end_bc):
    radius, inward, outward, axial = radial
    last_radial = radius.shape[0] - 1
    radial_ids = jnp.arange(radius.shape[0], dtype=jnp.int32)
    open_out = (radial_ids[None, :] == last_radial) & (outer_bc[:, None] == 0)
    open_low = (axial_ids[:, None] == 0) & (end_bc[None, :] == 0)
    open_high = (axial_ids[:, None] == total_axial - 1) & (end_bc[None, :] == 0)
    baseline = inward[None, :] + outward[None, :] * jnp.where(open_out, 0.0, 1.0)
    baseline = baseline + axial * (jnp.where(open_low, 0.0, 1.0) + jnp.where(open_high, 0.0, 1.0))
    mode_order = jnp.minimum(mode_ids, NPHI - mode_ids).astype(jnp.float32)
    return (
        baseline[None] + (mode_order * mode_order)[:, None, None] / (radius * radius)[None, None, :]
    )


def neighbours(extended, radial):
    radius, inward, outward, axial = radial
    middle = extended[:, 1:-1, :]
    zero_edge = jnp.zeros_like(middle[:, :, :1])
    below_r = jnp.concatenate([zero_edge, middle[:, :, :-1]], axis=2)
    above_r = jnp.concatenate([middle[:, :, 1:], zero_edge], axis=2)
    return axial * (extended[:, 2:, :] + extended[:, :-2, :]) + inward * below_r + outward * above_r


def relax_step(extended, source, diag_part, radial):
    middle = extended[:, 1:-1, :]
    return (
        middle
        + relaxation * (source + neighbours(extended, radial) - diag_part * middle) / diag_part
    )


def operate(extended, diag_part, radial):
    return diag_part * extended[:, 1:-1, :] - neighbours(extended, radial)


def pad_axial(values):
    return jnp.pad(values, ((0, 0), (1, 1), (0, 0)))


def restrict(residual):
    modes, cells_z, cells_r = residual.shape
    return residual.reshape(modes, cells_z // 2, 2, cells_r // 2, 2).sum(axis=(2, 4)) * 0.25


def prolong(correction):
    return jnp.repeat(jnp.repeat(correction, 2, axis=1), 2, axis=2)


def body(charge, outer_held, end_held):
    hartley = hartley_table(NPHI)
    mode_count = charge.shape[0]
    cells_z = charge.shape[1]
    cells_r = charge.shape[2]
    total_z = cells_z * lax.axis_size("gz")
    spectrum_rows = transform_rows(
        hartley, lax.all_to_all(charge, "phi", split_axis=1, concat_axis=0, tiled=True)
    )
    spectrum = lax.all_to_all(spectrum_rows, "phi", split_axis=0, concat_axis=1, tiled=True)
    fine_terms = radial_terms(cells_r, False)
    coarse_terms = radial_terms(cells_r // 2, True)
    own = lax.all_to_all(spectrum, "gz", split_axis=0, concat_axis=1, tiled=True)
    few = own.shape[0]
    own_modes = (
        lax.axis_index("phi") * mode_count
        + lax.axis_index("gz") * few
        + jnp.arange(few, dtype=jnp.int32)
    )
    full_diag = diagonal(
        own_modes, jnp.arange(total_z, dtype=jnp.int32), total_z, fine_terms, outer_held, end_held
    )
    half_diag = diagonal(
        own_modes,
        jnp.arange(total_z // 2, dtype=jnp.int32),
        total_z // 2,
        coarse_terms,
        outer_held[0::2],
        end_held[0::2],
    )
    local_solution = jnp.zeros_like(own)
    local_rows = []
    for cycle_index in range(VCYC):
        for sweep_index in range(NU):
            local_solution = relax_step(pad_axial(local_solution), own, full_diag, fine_terms)
        residual = own - operate(pad_axial(local_solution), full_diag, fine_terms)
        coarse_rhs = restrict(residual)
        estimate = relaxation * coarse_rhs / half_diag
        for sweep_index in range(KC):
            estimate = relax_step(pad_axial(estimate), coarse_rhs, half_diag, coarse_terms)
        spread = prolong(estimate)
        image = operate(pad_axial(spread), full_diag, fine_terms)
        top = jnp.sum(residual * image, axis=(1, 2))
        bottom = jnp.sum(image * image, axis=(1, 2))
        factor = top / (bottom + small_floor)
        local_solution = local_solution + factor[:, None, None] * spread
        for sweep_index in range(NU):
            local_solution = relax_step(pad_axial(local_solution), own, full_diag, fine_terms)
        local_rows.append(factor)
    solution = lax.all_to_all(local_solution, "gz", split_axis=1, concat_axis=0, tiled=True)
    scales = lax.all_gather(jnp.stack(local_rows), "gz", axis=1, tiled=True)
    rows_back = transform_rows(
        hartley, lax.all_to_all(solution, "phi", split_axis=1, concat_axis=0, tiled=True)
    )
    potential = lax.all_to_all(rows_back, "phi", split_axis=0, concat_axis=1, tiled=True)
    return (potential, scales)


def solution(mesh):
    in_specs = (P("phi", "gz", None), P(), P())
    out_specs = (P("phi", "gz", None), P(None, "phi"))
    return jax.shard_map(body, mesh=mesh, in_specs=in_specs, out_specs=out_specs, check_vma=False)
```

profile of v0, /device:TPU:1, one launch (start us, length us, event | category | flops | bytes accessed | tf_op | source)
XLA Modules:
  0.0 393.6 jit_solution(18095182347208205018)
XLA Ops:
  0.6 1.8 copy.123
  2.5 38.3 %all_to_all.102 = f32[64,16,256]{2,0,1:T(8,128)S(1)} all-to-all(f32[64,16,256]{2,0,1:T(8,128)S(1)} %copy.123), channel_id=1, replica_groups=mesh['phi'=16,'gz'=16] {'phi'}, dimensions={1} | all-to-all | bytes 2097152 | tf_op jit(solution)/shard_map/all_to_all | solution.py:99
  40.8 36.6 %fusion.8 = f32[1024,1,256]{2,0,1:T(8,128)S(1)} fusion(f32[1024,256]{1,0:T(8,128)S(1)} %bitcast.88), kind=kOutput, calls=%fused_computation.46 | convolution fusion | flops 3238002688 | bytes 2097152 | tf_op jit(solution)/shard_map/dot_general | solution.py:28
  77.4 2.0 copy.124
  79.4 3.6 all-to-all-start.1
  83.0 0.2 slice.270
  83.2 0.2 slice.271
  83.7 26.6 %all-to-all-done.1 = f32[1024,1,256]{2,1,0:T(1,128)S(1)} async-done(((f32[1024,1,256]{2,1,0:T(1,128)}), f32[1024,1,256]{2,1,0:T(1,128)S(1)}, u32[]{:S(2)}, u32[]{:S(2)}) %all-to-all-start.1) | async-done | bytes 1048608 | tf_op jit(solution)/shard_map/all_to_all | solution.py:101
  110.3 1.6 copy.125
  111.9 6.8 %all-to-all-start.2 = ((f32[64,16,256]{2,1,0:T(8,128)}), f32[64,16,256]{2,1,0:T(8,128)S(1)}, u32[]{:S(2)}, u32[]{:S(2)}) async-start(f32[64,16,256]{2,1,0:T(8,128)} %copy.125), calls=%async_computation.2 | async-start | bytes 2097152 | tf_op jit(solution)/shard_map/all_to_all | solution.py:104
  119.2 18.5 %all-to-all-done.2 = f32[64,16,256]{2,1,0:T(8,128)S(1)} async-done(((f32[64,16,256]{2,1,0:T(8,128)}), f32[64,16,256]{2,1,0:T(8,128)S(1)}, u32[]{:S(2)}, u32[]{:S(2)}) %all-to-all-start.2) | async-done | bytes 1048608 | tf_op jit(solution)/shard_map/all_to_all | solution.py:104
  137.8 0.3 add_divide_fusion.7
  138.1 0.4 fusion.116
  138.4 0.7 fusion.14
  139.1 0.4 fusion.115
  139.5 0.6 fusion.16
  140.1 16.9 %copy.127 = f32[4,256,256]{0,2,1:T(8,128)} copy(f32[4,256,256]{2,1,0:T(8,128)S(1)} %fusion.16) | data formatting | bytes 2097152 | tf_op jit(solution)/shard_map/sub | solution.py:127
  156.9 32.2 %reduce_sum.54 = f32[4,128,128]{0,2,1:T(8,128)} reduce(f32[4,128,2,128,2]{0,4,3,2,1:T(2,128)} %bitcast.77, f32[]{:T(128)} %constant.34.clone.1), dimensions={2,4}, to_apply=%region_0.1 | reduce | flops 196608 | bytes 1310724 | tf_op jit(solution)/shard_map/reduce_sum | solution.py:85
  189.1 5.4 %copy.128 = f32[4,128,128]{2,1,0:T(8,128)S(1)} copy(f32[4,128,128]{0,2,1:T(8,128)} %reduce_sum.54) | data formatting | bytes 524288 | tf_op jit(solution)/shard_map/reduce_sum | solution.py:85
  194.7 0.2 fusion.81
  195.1 0.2 fusion.82
  195.4 0.2 fusion.83
  195.8 0.2 copy.130
  196.1 1.1 broadcast_in_dim.40
  197.2 1.6 copy.131
  198.8 0.3 fusion.114
  199.1 0.9 copy-done.3
  200.0 0.8 multiply_reduce_fusion.2
  200.9 0.4 fusion.113
  201.3 0.7 fusion.20
  202.0 0.4 fusion.112
  202.4 0.7 fusion.23
  203.1 0.4 fusion.111
  203.4 0.7 fusion.26
  204.1 0.4 fusion.110
  204.5 0.7 fusion.29
  205.2 0.4 fusion.109
  205.5 0.6 fusion.31
  206.1 16.9 %copy.136 = f32[4,256,256]{0,2,1:T(8,128)} copy(f32[4,256,256]{2,1,0:T(8,128)S(1)} %fusion.31) | data formatting | bytes 2097152 | tf_op jit(solution)/shard_map/sub | solution.py:127
  223.0 32.2 %reduce_sum.57 = f32[4,128,128]{0,2,1:T(8,128)} reduce(f32[4,128,2,128,2]{0,4,3,2,1:T(2,128)} %bitcast.76, f32[]{:T(128)} %constant.34.clone.1), dimensions={2,4}, to_apply=%region_3.4 | reduce | flops 196608 | bytes 1310724 | tf_op jit(solution)/shard_map/reduce_sum | solution.py:85
  255.2 5.4 %copy.137 = f32[4,128,128]{2,1,0:T(8,128)S(1)} copy(f32[4,128,128]{0,2,1:T(8,128)} %reduce_sum.57) | data formatting | bytes 524288 | tf_op jit(solution)/shard_map/reduce_sum | solution.py:85
  261.2 0.2 fusion.85
  261.5 0.2 fusion.86
  261.9 0.2 copy.139
  262.2 1.1 broadcast_in_dim.42
  263.3 1.6 copy.140
  264.9 0.3 fusion.108
  265.2 0.9 copy-done.1
  266.1 0.8 multiply_reduce_fusion
  267.0 0.4 fusion.107
  267.4 0.7 fusion.35
  268.1 0.4 fusion.106
  268.5 0.7 fusion.38
  269.1 0.7 copy.145
  269.8 19.3 %all_to_all.103 = f32[4,256,256]{2,0,1:T(4,128)S(1)} all-to-all(f32[4,256,256]{2,0,1:T(4,128)S(1)} %copy.145), channel_id=1, replica_groups=mesh['phi'=16,'gz'=16] {'gz'}, dimensions={1} | all-to-all | bytes 2097152 | tf_op jit(solution)/shard_map/all_to_all | solution.py:141
  289.4 0.6 copy.148
  290.0 32.5 %all_to_all.104 = f32[64,16,256]{2,0,1:T(8,128)S(1)} all-to-all(f32[64,16,256]{2,0,1:T(8,128)S(1)} %copy.148), channel_id=1, replica_groups=mesh['phi'=16,'gz'=16] {'phi'}, dimensions={1} | all-to-all | bytes 2097152 | tf_op jit(solution)/shard_map/all_to_all | solution.py:144
  322.6 36.6 %fusion.9 = f32[1024,1,256]{2,0,1:T(8,128)S(1)} fusion(f32[1024,256]{1,0:T(8,128)S(1)} %bitcast.89), kind=kOutput, calls=%fused_computation.47 | convolution fusion | flops 3238002688 | bytes 2097152 | tf_op jit(solution)/shard_map/dot_general | solution.py:28
  359.1 2.0 copy.149
  361.2 3.6 all-to-all-start.5
  364.7 17.3 %all-gather = f32[16,4,2]{1,2,0:T(2,128)S(1)} all-gather(f32[1,4,2]{1,2,0:T(2,128)S(1)} %maximum_bitcast_fusion), channel_id=1, replica_groups=mesh['phi'=16,'gz'=16] {'gz'}, dimensions={0}, use_global_device_ids=true | all-gather | bytes 544 | tf_op jit(solution)/shard_map/all_gather | solution.py:142
  382.1 0.7 reshape.481
  382.7 9.3 %all-to-all-done.5 = f32[1024,1,256]{2,1,0:T(1,128)S(1)} async-done(((f32[1024,1,256]{2,1,0:T(1,128)}), f32[1024,1,256]{2,1,0:T(1,128)S(1)}, u32[]{:S(2)}, u32[]{:S(2)}) %all-to-all-start.5) | async-done | bytes 1048608 | tf_op jit(solution)/shard_map/all_to_all | solution.py:146
  392.0 1.6 copy.154
  (48 shorter events, 2.9 us)
Async XLA Ops:
  77.4 5.6 %copy-start.5 = (s32[256]{0:T(256)S(1)}, s32[256]{0:T(256)}, u32[]{:S(2)}) copy-start(s32[256]{0:T(256)} %param.4) | copy-start | bytes 3076
  77.4 5.9 %copy-start.4 = (s32[256]{0:T(256)S(1)}, s32[256]{0:T(256)}, u32[]{:S(2)}) copy-start(s32[256]{0:T(256)} %param.5) | copy-start | bytes 3076
  79.4 30.8 %all-to-all-start.1 = ((f32[1024,1,256]{2,1,0:T(1,128)}), f32[1024,1,256]{2,1,0:T(1,128)S(1)}, u32[]{:S(2)}, u32[]{:S(2)}) async-start(f32[1024,1,256]{2,1,0:T(1,128)} %copy.124), calls=%async_computation.1 | async-start | bytes 2097152 | tf_op jit(solution)/shard_map/all_to_all | solution.py:101
  111.9 25.7 %all-to-all-start.2 = ((f32[64,16,256]{2,1,0:T(8,128)}), f32[64,16,256]{2,1,0:T(8,128)S(1)}, u32[]{:S(2)}, u32[]{:S(2)}) async-start(f32[64,16,256]{2,1,0:T(8,128)} %copy.125), calls=%async_computation.2 | async-start | bytes 2097152 | tf_op jit(solution)/shard_map/all_to_all | solution.py:104
  140.1 16.9 %copy-start.2 = (f32[4,256,256]{2,1,0:T(8,128)}, f32[4,256,256]{2,1,0:T(8,128)S(1)}, u32[]{:S(2)}) copy-start(f32[4,256,256]{2,1,0:T(8,128)S(1)} %fusion.16) | copy-start | bytes 3145732
  198.8 1.2 copy-start.3
  206.1 16.9 %copy-start = (f32[4,256,256]{2,1,0:T(8,128)}, f32[4,256,256]{2,1,0:T(8,128)S(1)}, u32[]{:S(2)}) copy-start(f32[4,256,256]{2,1,0:T(8,128)S(1)} %fusion.31) | copy-start | bytes 3145732
  264.8 1.2 copy-start.1
  361.2 30.9 %all-to-all-start.5 = ((f32[1024,1,256]{2,1,0:T(1,128)}), f32[1024,1,256]{2,1,0:T(1,128)S(1)}, u32[]{:S(2)}, u32[]{:S(2)}) async-start(f32[1024,1,256]{2,1,0:T(1,128)} %copy.149), calls=%async_computation.5 | async-start | bytes 2097152 | tf_op jit(solution)/shard_map/all_to_all | solution.py:146
where the time goes:
time: 394 us
  blocking collectives  107 us (27%)
  other arithmetic  74.6 us (19%)
  matrix products  73.1 us (19%)
  local copies, waits for them, and re-layouts  69.1 us (18%)
  waiting for transfers between devices  54.4 us (14%)
  starting transfers between devices  13.9 us (4%)
    dot_general x2, matrix products, transform_rows(): jnp.dot(hartley, flat, precision=lax.Precision.HIGHEST, preferred_element...  73.1 us
    reduce_sum x2, other arithmetic, restrict(): residual.reshape(modes, cells_z // 2, 2, cells_r // 2, 2).sum(axis=(2, 4))  64.4 us
    all_to_all x1, blocking collectives, body(): lax.all_to_all(charge, 'phi', split_axis=1, concat_axis=0, tiled=True)  38.3 us
    sub x2, local copies, waits for them, and re-layouts, body(): residual = own - operate(pad_axial(local_solution), full_diag, fine_terms)  33.7 us
    all_to_all x1, blocking collectives, body(): lax.all_to_all(solution, 'phi', split_axis=1, concat_axis=0, tiled=True)  32.5 us
    all_to_all x1, waiting for transfers between devices, body(): lax.all_to_all(spectrum_rows, 'phi', split_axis=0, concat_axis=1, tiled=T...  26.6 us
    all_to_all x1, blocking collectives, body(): lax.all_to_all(local_solution, 'gz', split_axis=1, concat_axis=0, tiled=T...  19.3 us
    all_to_all x1, waiting for transfers between devices, body(): lax.all_to_all(spectrum, 'gz', split_axis=0, concat_axis=1, tiled=True)  18.5 us
  transfers between devices with their start and end apart: 3, of which 3 were waited for; matrix products, arithmetic and copies ran while one was open for 0% of the time, Pallas kernels for 0%

commit v1 on v0

v1 whole, which is shorter than its diff:
```python
import functools
import math

import jax
import jax.numpy as jnp
import numpy as np
from jax import lax
from jax.experimental import pallas as pl
from jax.experimental.pallas import tpu as pltpu
from jax.sharding import PartitionSpec as P

NPHI = 1024
VCYC = 2
NU = 2
KC = 3
RIN = 131
NR = 256
NZ = 256
HALF = 128
FEW = 4

relaxation = 0.8
small_floor = 1e-06
f32 = jnp.float32
bf16 = jnp.bfloat16

PAD = 8
CH = 32


def hartley_tables():
    k = np.arange(NPHI)
    phase = (np.outer(k, k) % NPHI) * (2.0 * math.pi / NPHI)
    table = ((np.cos(phase) + np.sin(phase)) / math.sqrt(NPHI)).astype(np.float32)
    high = table.astype(jnp.bfloat16)
    low = (table - high.astype(np.float32)).astype(jnp.bfloat16)
    return high, low


def parity_table():
    perm = np.zeros((NR, NR), np.float32)
    i = np.arange(NR)
    perm[i, (i % 2) * HALF + i // 2] = 1.0
    return perm.astype(jnp.bfloat16)


def split(values):
    high = values.astype(bf16)
    low = (values - high.astype(f32)).astype(bf16)
    return high, low


def transform_kernel(high_ref, low_ref, perm_ref, x_ref, o_ref, xh, xl):
    for piece in range(4):
        rows = pl.ds(piece * 256, 256)
        h, l = split(x_ref[rows, :])
        xh[rows, :] = jnp.dot(h, perm_ref[...], preferred_element_type=f32).astype(bf16)
        xl[rows, :] = jnp.dot(l, perm_ref[...], preferred_element_type=f32).astype(bf16)
    for piece in range(4):
        rows = pl.ds(piece * 256, 256)
        acc = jnp.dot(high_ref[rows, :], xh[...], preferred_element_type=f32)
        acc += jnp.dot(high_ref[rows, :], xl[...], preferred_element_type=f32)
        acc += jnp.dot(low_ref[rows, :], xh[...], preferred_element_type=f32)
        o_ref[rows, :] = acc


def transform(high, low, perm, x):
    return pl.pallas_call(
        transform_kernel,
        out_shape=jax.ShapeDtypeStruct((NPHI, NR), f32),
        scratch_shapes=[pltpu.VMEM((NPHI, NR), bf16), pltpu.VMEM((NPHI, NR), bf16)],
        compiler_params=pltpu.CompilerParams(vmem_limit_bytes=32 << 20),
        cost_estimate=pl.CostEstimate(
            flops=6 * NPHI * NPHI * NR, bytes_accessed=6 << 20, transcendentals=0
        ),
        name="transform",
    )(high, low, perm, x)


def lane_ids(rows=1):
    return lax.broadcasted_iota(jnp.int32, (rows, HALF), 1)


def fine_rows(parity):
    i = 2 * lane_ids() + parity
    radius = i.astype(f32) + (RIN + 0.5)
    inward = (radius - 0.5) / radius
    outward = (radius + 0.5) / radius
    return radius, inward, outward


def coarse_rows():
    radius = 2.0 * lane_ids().astype(f32) + (RIN + 1.0)
    inward = (radius - 1.0) / (4.0 * radius)
    outward = (radius + 1.0) / (4.0 * radius)
    return radius, inward, outward


def as_column(row):
    square = jnp.broadcast_to(row, (HALF, HALF))
    diag = lax.broadcasted_iota(jnp.int32, (HALF, HALF), 0) == lane_ids(HALF)
    return jnp.sum(jnp.where(diag, square, 0.0), axis=1, keepdims=True)


def setup_base(base_ref, outer_rows, end_rows):
    y = lax.broadcasted_iota(jnp.int32, (HALF, HALF), 0)
    j = lane_ids(HALF)
    for zp in range(2):
        open_outer = 1.0 - as_column(outer_rows[zp])
        for ip in range(2):
            _, inward, outward = fine_rows(ip)
            open_end = 1.0 - end_rows[ip]
            value = jnp.broadcast_to(inward + outward + 2.0, (HALF, HALF))
            if ip == 1:
                value = value - jnp.where(j == HALF - 1, outward * open_outer, 0.0)
            edge = 0 if zp == 0 else HALF - 1
            value = value - jnp.where(y == edge, open_end, 0.0)
            base_ref[2 * zp + ip] = value
    _, inward, outward = coarse_rows()
    open_outer = 1.0 - as_column(outer_rows[0])
    open_end = 1.0 - end_rows[0]
    value = jnp.broadcast_to(inward + outward + 0.5, (HALF, HALF))
    value = value - jnp.where(j == HALF - 1, outward * open_outer, 0.0)
    value = value - jnp.where((y == 0) | (y == HALF - 1), 0.25 * open_end, 0.0)
    base_ref[4] = value


def left_of(value):
    return pltpu.roll(value, 1, 1)


def right_of(value):
    return pltpu.roll(value, HALF - 1, 1)


def solve_mode(mode, f_ref, base_ref, d_ref, w_ref, va, vb, r_ref, ca, cb, cr_ref, write):
    order = jnp.minimum(mode, NPHI - mode).astype(f32)
    square = order * order
    rows_e = fine_rows(0)
    rows_o = fine_rows(1)
    first = lane_ids() == 0
    last = lane_ids() == HALF - 1
    in_e = jnp.where(first, 0.0, rows_e[1])
    out_e = rows_e[2]
    in_o = rows_o[1]
    out_o = jnp.where(last, 0.0, rows_o[2])
    radius_c, in_c0, out_c0 = coarse_rows()
    in_c = jnp.where(first, 0.0, in_c0)
    out_c = jnp.where(last, 0.0, out_c0)
    term_e = square / (rows_e[0] * rows_e[0])
    term_o = square / (rows_o[0] * rows_o[0])
    term_c = square / (radius_c * radius_c)
    chunks = [pl.ds(s, CH) for s in range(0, HALF, CH)]
    padded = [pl.ds(PAD + s, CH) for s in range(0, HALF, CH)]
    above = [pl.ds(PAD + s - 1, CH) for s in range(0, HALF, CH)]
    below = [pl.ds(PAD + s + 1, CH) for s in range(0, HALF, CH)]
    count = len(chunks)

    def neighbours(v, c):
        ee, eo, oe, oo = (v[q, padded[c], :] for q in range(4))
        oe_up, oo_up = v[2, above[c], :], v[3, above[c], :]
        ee_dn, eo_dn = v[0, below[c], :], v[1, below[c], :]
        n_ee = (oe_up + oe) + (in_e * left_of(eo) + out_e * eo)
        n_eo = (oo_up + oo) + (in_o * ee + out_o * right_of(ee))
        n_oe = (ee + ee_dn) + (in_e * left_of(oo) + out_e * oo)
        n_oo = (eo + eo_dn) + (in_o * oe + out_o * right_of(oe))
        return (ee, eo, oe, oo), (n_ee, n_eo, n_oe, n_oo)

    def sweep(src, dst, emit=None):
        for c in range(count):
            centre, near = neighbours(src, c)
            for q in range(4):
                value = (1.0 - relaxation) * centre[q] + w_ref[q, chunks[c], :] * (
                    f_ref[q, chunks[c], :] + near[q]
                )
                if emit is None:
                    dst[q, padded[c], :] = value
                else:
                    emit(q, c * CH, value)

    for c in range(count):
        for q in range(4):
            d = base_ref[q, chunks[c], :] + (term_e if q % 2 == 0 else term_o)
            w = relaxation / d
            d_ref[q, chunks[c], :] = d
            w_ref[q, chunks[c], :] = w
            va[q, padded[c], :] = w * f_ref[q, chunks[c], :]
        d_ref[4, chunks[c], :] = relaxation / (base_ref[4, chunks[c], :] + term_c)

    factors = []
    cur, other = va, vb
    for cycle in range(VCYC):
        for s in range(1 if cycle == 0 else 0, NU):
            sweep(cur, other)
            cur, other = other, cur
        for c in range(count):
            centre, near = neighbours(cur, c)
            total = None
            for q in range(4):
                res = f_ref[q, chunks[c], :] + near[q] - d_ref[q, chunks[c], :] * centre[q]
                r_ref[q, chunks[c], :] = res
                total = res if total is None else total + res
            total = total * 0.25
            cr_ref[chunks[c], :] = total
            ca[padded[c], :] = d_ref[4, chunks[c], :] * total
        now, later = ca, cb
        for s in range(KC):
            for c in range(count):
                w = now[padded[c], :]
                near = (
                    in_c * left_of(w)
                    + out_c * right_of(w)
                    + 0.25 * (now[above[c], :] + now[below[c], :])
                )
                later[padded[c], :] = (1.0 - relaxation) * w + d_ref[4, chunks[c], :] * (
                    cr_ref[chunks[c], :] + near
                )
            now, later = later, now
        top = jnp.zeros((8, HALF), f32)
        bottom = jnp.zeros((8, HALF), f32)
        for c in range(count):
            w = now[padded[c], :]
            low_e = in_e * left_of(w) + out_e * w
            low_o = in_o * w + out_o * right_of(w)
            up = now[above[c], :] + w
            down = now[below[c], :] + w
            for q in range(4):
                image = d_ref[q, chunks[c], :] * w - (low_e if q % 2 == 0 else low_o)
                image = image - (up if q < 2 else down)
                res = r_ref[q, chunks[c], :]
                for g in range(CH // 8):
                    part = image[8 * g : 8 * g + 8]
                    top = top + res[8 * g : 8 * g + 8] * part
                    bottom = bottom + part * part
        factor = jnp.sum(top, keepdims=True) / (jnp.sum(bottom, keepdims=True) + small_floor)
        factors.append(factor)
        for c in range(count):
            add = factor * now[padded[c], :]
            for q in range(4):
                cur[q, padded[c], :] = cur[q, padded[c], :] + add
        for s in range(NU):
            if cycle == VCYC - 1 and s == NU - 1:
                sweep(cur, None, write)
            else:
                sweep(cur, other)
                cur, other = other, cur
    return factors


def solve_kernel(outer_ref, end_ref, perm_ref, f_ref, o_ref, s_ref, f, base, d, w, va, vb, r, ca, cb, cr, flat):
    step = pl.program_id(0)

    @pl.when(step == 0)
    def _():
        held = jnp.concatenate([outer_ref[...], end_ref[...]], axis=0).astype(f32).astype(bf16)
        held = jnp.concatenate([held] * 8, axis=0)
        held = jnp.dot(held, perm_ref[...], preferred_element_type=f32)
        outer_rows = [held[0:1, :HALF], held[0:1, HALF:]]
        end_rows = [held[1:2, :HALF], held[1:2, HALF:]]
        setup_base(base, outer_rows, end_rows)
        for ref in (va, vb):
            ref[:, 0:PAD, :] = jnp.zeros((4, PAD, HALF), f32)
            ref[:, HALF + PAD :, :] = jnp.zeros((4, PAD, HALF), f32)
        for ref in (ca, cb):
            ref[0:PAD, :] = jnp.zeros((PAD, HALF), f32)
            ref[HALF + PAD :, :] = jnp.zeros((PAD, HALF), f32)

    mode = (lax.axis_index("phi") * 16 + lax.axis_index("gz")) * FEW + step
    for ip in range(2):
        flat[ip] = f_ref[0, :, ip * HALF : (ip + 1) * HALF]
    for q in range(4):
        f[q] = flat[q % 2, pl.ds(q // 2, HALF, stride=2), :]

    def write(q, start, value):
        flat[q % 2, pl.ds(2 * start + q // 2, CH, stride=2), :] = value

    factors = solve_mode(mode, f, base, d, w, va, vb, r, ca, cb, cr, write)
    for ip in range(2):
        o_ref[0, :, ip * HALF : (ip + 1) * HALF] = flat[ip]
    for cycle in range(VCYC):
        s_ref[0, cycle : cycle + 1, :] = jnp.broadcast_to(factors[cycle], (1, HALF))


def solve(outer, end, perm, own):
    quad = lambda n: pltpu.VMEM((n, HALF, HALF), f32)
    return pl.pallas_call(
        solve_kernel,
        grid=(FEW,),
        out_shape=(
            jax.ShapeDtypeStruct((FEW, NZ, NR), f32),
            jax.ShapeDtypeStruct((FEW, 8, HALF), f32),
        ),
        in_specs=[
            pl.BlockSpec((1, NZ), lambda m: (0, 0)),
            pl.BlockSpec((1, NR), lambda m: (0, 0)),
            pl.BlockSpec((NR, NR), lambda m: (0, 0)),
            pl.BlockSpec((1, NZ, NR), lambda m: (m, 0, 0)),
        ],
        out_specs=(
            pl.BlockSpec((1, NZ, NR), lambda m: (m, 0, 0)),
            pl.BlockSpec((1, 8, HALF), lambda m: (m, 0, 0)),
        ),
        scratch_shapes=[
            quad(4), quad(5), quad(5), quad(4),
            pltpu.VMEM((4, HALF + 2 * PAD, HALF), f32),
            pltpu.VMEM((4, HALF + 2 * PAD, HALF), f32),
            quad(4),
            pltpu.VMEM((HALF + 2 * PAD, HALF), f32),
            pltpu.VMEM((HALF + 2 * PAD, HALF), f32),
            pltpu.VMEM((HALF, HALF), f32),
            pltpu.VMEM((2, NZ, HALF), f32),
        ],
        compiler_params=pltpu.CompilerParams(vmem_limit_bytes=32 << 20),
        cost_estimate=pl.CostEstimate(
            flops=200 * FEW * NZ * NR, bytes_accessed=2 << 20, transcendentals=0
        ),
        name="solve",
    )(outer, end, perm, own)


def body(tables, charge, outer_held, end_held):
    high, low, forward, backward = (jnp.asarray(t) for t in tables)
    rows = lax.all_to_all(charge, "phi", split_axis=1, concat_axis=0, tiled=True)
    spectrum = transform(high, low, forward, rows.reshape(NPHI, NR)).reshape(NPHI, 1, NR)
    spectrum = lax.all_to_all(spectrum, "phi", split_axis=0, concat_axis=1, tiled=True)
    own = lax.all_to_all(spectrum, "gz", split_axis=0, concat_axis=1, tiled=True)
    outer = outer_held.reshape(1, NZ)
    end = end_held.reshape(1, NR)
    local, scale_rows = solve(outer, end, forward, own)
    mine = jnp.transpose(scale_rows[:, :VCYC, 0])
    scales = lax.all_gather(mine, "gz", axis=1, tiled=True)
    back = lax.all_to_all(local, "gz", split_axis=1, concat_axis=0, tiled=True)
    back = lax.all_to_all(back, "phi", split_axis=1, concat_axis=0, tiled=True)
    rows_back = transform(high, low, backward, back.reshape(NPHI, NR)).reshape(NPHI, 1, NR)
    potential = lax.all_to_all(rows_back, "phi", split_axis=0, concat_axis=1, tiled=True)
    return (potential, scales)


def solution(mesh):
    in_specs = (P("phi", "gz", None), P(), P())
    out_specs = (P("phi", "gz", None), P(None, "phi"))
    high, low = hartley_tables()
    perm = parity_table()
    tables = (high, low, perm, np.ascontiguousarray(perm.T))
    return jax.shard_map(
        functools.partial(body, tables), mesh=mesh, in_specs=in_specs, out_specs=out_specs, check_vma=False
    )
```

time: 394 us -> 202 us (0.51)
  other arithmetic: 74.6 us -> 0 us
  matrix products: 73.1 us -> 0 us
  local copies, waits for them, and re-layouts: 69.1 us -> 11.4 us
  blocking collectives: 107 us -> 164 us
  waiting for transfers between devices: 54.4 us -> 9.17 us
  Pallas kernels: 0 us -> 12.6 us
  starting transfers between devices: 13.9 us -> 3.55 us
    dot_general x2 -> x0, matrix products: 73.1 us -> none  [transform_rows(): jnp.dot(hartley, flat, precision=lax.Precision.HIGHEST, preferred_element...]
    reduce_sum x4 -> x0, other arithmetic: 65.9 us -> none  [the longest x2 64.4 us: restrict(): residual.reshape(modes, cells_z // 2, 2, cells_r // 2, 2).sum(axis=(2, 4))]
    all_to_all x2 -> x4, blocking collectives: 51.8 us -> 108 us  [the longest x1 34.2 us: body(): back = lax.all_to_all(back, 'phi', split_axis=1, concat_axis=0, tiled=True)]
    all_to_all x2 -> x0, waiting for transfers between devices: 45.1 us -> none  [the longest x1 26.6 us: body(): lax.all_to_all(spectrum_rows, 'phi', split_axis=0, concat_axis=1, tiled=T...]
    sub x2 -> x0, local copies, waits for them, and re-layouts: 33.7 us -> none  [body(): residual = own - operate(pad_axial(local_solution), full_diag, fine_terms)]
    pallas_call x0 -> x3, Pallas kernels: none -> 12.6 us  [the longest x1 8.51 us: solve(): pl.pallas_call(solve_kernel, grid=(FEW,), out_shape=(jax.ShapeDtypeStruct...]
    reduce_sum x2 -> x0, local copies, waits for them, and re-layouts: 10.8 us -> none  [restrict(): residual.reshape(modes, cells_z // 2, 2, cells_r // 2, 2).sum(axis=(2, 4))]
    all_to_all x2 -> x0, starting transfers between devices: 10.3 us -> none  [the longest x1 6.75 us: body(): lax.all_to_all(spectrum, 'gz', split_axis=0, concat_axis=1, tiled=True)]
  transfers between devices with their start and end apart: 3 -> 1, of which waited for: 3 -> 1; matrix products, arithmetic and copies ran while one was open for 0% -> 0% of each run, Pallas kernels for 0% -> 0%
where the time goes in v1:
time: 202 us; the launch traced here: 201 us
  blocking collectives  164 us (81%)
  Pallas kernels  12.6 us (6%)
  local copies, waits for them, and re-layouts  11.4 us (6%)
  waiting for transfers between devices  9.17 us (5%)
  starting transfers between devices  3.55 us (2%)
    all_to_all x1, blocking collectives, body(): lax.all_to_all(charge, 'phi', split_axis=1, concat_axis=0, tiled=True)  38.3 us
    all_to_all x1, blocking collectives, body(): back = lax.all_to_all(back, 'phi', split_axis=1, concat_axis=0, tiled=True)  34.2 us
    all_to_all x1, blocking collectives, body(): lax.all_to_all(spectrum, 'phi', split_axis=0, concat_axis=1, tiled=True)  31.3 us
    all_to_all x1, blocking collectives, body(): lax.all_to_all(spectrum, 'gz', split_axis=0, concat_axis=1, tiled=True)  23.6 us
    all_to_all x1, blocking collectives, body(): back = lax.all_to_all(local, 'gz', split_axis=1, concat_axis=0, tiled=True)  18.9 us
    all_gather x1, blocking collectives, body(): scales = lax.all_gather(mine, 'gz', axis=1, tiled=True)  17.3 us
    all_to_all x1, waiting for transfers between devices, body(): lax.all_to_all(rows_back, 'phi', split_axis=0, concat_axis=1, tiled=True)  9.17 us
    pallas_call x1, Pallas kernels, solve(): pl.pallas_call(solve_kernel, grid=(FEW,), out_shape=(jax.ShapeDtypeStruct...  8.51 us
  transfers between devices with their start and end apart: 1, of which 1 were waited for; matrix products, arithmetic and copies ran while one was open for 0% of the time, Pallas kernels for 0%

profile of v1, /device:TPU:1, one launch (start us, length us, event | category | flops | bytes accessed | tf_op | source)
XLA Modules:
  0.0 201.1 jit_solution(548847665357483793)
XLA Ops:
  0.6 0.0 copy-start
  0.6 0.0 copy-start.1
  0.7 2.0 copy.40
  2.6 38.3 %all_to_all.102 = f32[64,16,256]{2,0,1:T(8,128)S(1)} all-to-all(f32[64,16,256]{2,0,1:T(8,128)S(1)} %copy.40), channel_id=1, replica_groups=mesh['phi'=16,'gz'=16] {'phi'}, dimensions={1} | all-to-all | bytes 2097152 | tf_op jit(solution)/shard_map/all_to_all | solution.py:323
  41.0 0.0 copy-done
  41.0 0.0 copy-done.1
  41.0 0.0 copy-start.3
  41.0 0.9 copy-done.3
  41.9 2.1 %transform.2 = f32[1024,256]{1,0:T(8,128)S(1)} custom-call(bf16[1024,1024]{1,0:T(8,128)(2,1)S(1)} %copy-done.1, bf16[1024,1024]{1,0:T(8,128)(2,1)S(1)} %copy-done, bf16[256,256]{1,0:T(8,128)(2,1)S(1)} %copy-done.3, f32[1024,256]{1,0:T(8,128)S(1)} %bitcast.40), custom_call_target="tpu_custom_call" | custom-call | flops 1610612736 | bytes 6291456 | tf_op jit(solution)/shard_map/transform/pallas_call | solution.py:68
  43.9 1.1 copy.41
  45.0 31.3 %all_to_all.103 = f32[1024,1,256]{2,1,0:T(1,128)S(1)} all-to-all(f32[1024,1,256]{2,1,0:T(1,128)S(1)} %copy.41), channel_id=1, replica_groups=mesh['phi'=16,'gz'=16] {'phi'}, dimensions={0} | all-to-all | bytes 2097152 | tf_op jit(solution)/shard_map/all_to_all | solution.py:325
  76.3 0.1 copy.50
  76.4 0.6 copy.42
  77.0 0.0 copy-start.5
  77.0 0.0 copy-start.6
  77.0 23.6 %all_to_all.104 = f32[64,16,256]{2,1,0:T(8,128)S(1)} all-to-all(f32[64,16,256]{2,1,0:T(8,128)S(1)} %copy.42), channel_id=1, replica_groups=mesh['phi'=16,'gz'=16] {'gz'}, dimensions={0} | all-to-all | bytes 2097152 | tf_op jit(solution)/shard_map/all_to_all | solution.py:326
  100.6 0.1 copy.43
  100.7 0.0 copy-done.5
  100.7 0.0 copy-done.6
  100.7 8.5 %solve.1 = (f32[4,256,256]{2,1,0:T(8,128)S(1)}, f32[4,8,128]{2,1,0:T(8,128)S(1)}) custom-call(s32[1,256]{1,0:T(1,128)S(1)} %bitcast.43, s32[1,256]{1,0:T(1,128)S(1)} %bitcast.44, bf16[256,256]{1,0:T(8,128)(2,1)S(1)} %copy-done.3, f32[4,256,256]{2,1,0:T(8,128)S(1)} %bitcast.42), custom_call_target="tpu_custom_call" | custom-call | flops 52428800 | bytes 2097152 | tf_op jit(solution)/shard_map/solve/pallas_call | solution.py:286
  109.2 0.7 copy.44
  109.9 18.9 %all_to_all.105 = f32[4,256,256]{2,0,1:T(4,128)S(1)} all-to-all(f32[4,256,256]{2,0,1:T(4,128)S(1)} %copy.44), channel_id=1, replica_groups=mesh['phi'=16,'gz'=16] {'gz'}, dimensions={1} | all-to-all | bytes 2097152 | tf_op jit(solution)/shard_map/all_to_all | solution.py:332
  128.7 0.3 copy.45
  129.0 0.0 copy-start.4
  129.0 1.3 all_to_all.88
  130.3 0.0 copy-start.2
  130.3 34.2 %all_to_all.106 = f32[64,16,256]{2,0,1:T(8,128)S(1)} all-to-all(f32[64,16,256]{2,0,1:T(8,128)} %all_to_all.88), channel_id=1, replica_groups=mesh['phi'=16,'gz'=16] {'phi'}, dimensions={1} | all-to-all | bytes 2097152 | tf_op jit(solution)/shard_map/all_to_all | solution.py:333
  164.5 0.0 copy-done.4
  164.5 0.0 copy-done.2
  164.5 2.1 %transform.3 = f32[1024,256]{1,0:T(8,128)S(1)} custom-call(bf16[1024,1024]{1,0:T(8,128)(2,1)S(1)} %copy-done.2, bf16[1024,1024]{1,0:T(8,128)(2,1)S(1)} %copy-done, bf16[256,256]{1,0:T(8,128)(2,1)S(1)} %copy-done.4, f32[1024,256]{1,0:T(8,128)S(1)} %bitcast.38), custom_call_target="tpu_custom_call" | custom-call | flops 1610612736 | bytes 6291456 | tf_op jit(solution)/shard_map/transform/pallas_call | solution.py:68
  166.6 2.1 %copy.46 = f32[1024,1,256]{2,1,0:T(1,128)} copy(f32[1024,1,256]{2,0,1:T(8,128)S(1)} %bitcast.39) | data formatting | bytes 2097152 | tf_op jit(solution)/shard_map/reshape | solution.py:334
  168.7 3.6 %all-to-all-start.5 = ((f32[1024,1,256]{2,1,0:T(1,128)}), f32[1024,1,256]{2,1,0:T(1,128)S(1)}, u32[]{:S(2)}, u32[]{:S(2)}) async-start(f32[1024,1,256]{2,1,0:T(1,128)} %copy.46), calls=%async_computation.5 | async-start | bytes 2097152 | tf_op jit(solution)/shard_map/all_to_all | solution.py:335
  172.2 0.1 copy.48
  172.3 17.3 %all-gather = f32[16,4,2]{1,2,0:T(2,128)S(1)} all-gather(f32[1,4,2]{1,2,0:T(2,128)S(1)} %bitcast.50), channel_id=1, replica_groups=mesh['phi'=16,'gz'=16] {'gz'}, dimensions={0}, use_global_device_ids=true | all-gather | bytes 544 | tf_op jit(solution)/shard_map/all_gather | solution.py:331
  189.7 0.7 reshape.31
  190.3 9.2 %all-to-all-done.5 = f32[1024,1,256]{2,1,0:T(1,128)S(1)} async-done(((f32[1024,1,256]{2,1,0:T(1,128)}), f32[1024,1,256]{2,1,0:T(1,128)S(1)}, u32[]{:S(2)}, u32[]{:S(2)}) %all-to-all-start.5) | async-done | bytes 1048608 | tf_op jit(solution)/shard_map/all_to_all | solution.py:335
  199.5 1.6 copy.52
  (2 shorter events, 0.0 us)
Async XLA Ops:
  0.6 40.3 %copy-start = (bf16[1024,1024]{1,0:T(8,128)(2,1)S(1)}, bf16[1024,1024]{1,0:T(8,128)(2,1)}, u32[]{:S(2)}) copy-start(bf16[1024,1024]{1,0:T(8,128)(2,1)} %constant.9.clone.low_ref) | copy-start | bytes 6291460
  0.6 40.3 %copy-start.1 = (bf16[1024,1024]{1,0:T(8,128)(2,1)S(1)}, bf16[1024,1024]{1,0:T(8,128)(2,1)}, u32[]{:S(2)}) copy-start(bf16[1024,1024]{1,0:T(8,128)(2,1)} %constant.8.clone.high_ref) | copy-start | bytes 6291460
  41.0 0.9 copy-start.3
  77.0 23.7 %copy-start.5 = (s32[256]{0:T(256)S(1)}, s32[256]{0:T(256)}, u32[]{:S(2)}) copy-start(s32[256]{0:T(256)} %param.8) | copy-start | bytes 3076
  77.0 23.7 %copy-start.6 = (s32[256]{0:T(256)S(1)}, s32[256]{0:T(256)}, u32[]{:S(2)}) copy-start(s32[256]{0:T(256)} %param.9) | copy-start | bytes 3076
  129.0 35.5 %copy-start.4 = (bf16[256,256]{1,0:T(8,128)(2,1)S(1)}, bf16[256,256]{1,0:T(8,128)(2,1)}, u32[]{:S(2)}) copy-start(bf16[256,256]{1,0:T(8,128)(2,1)} %constant.11.clone.perm_ref) | copy-start | bytes 393220
  130.3 34.2 %copy-start.2 = (bf16[1024,1024]{1,0:T(8,128)(2,1)S(1)}, bf16[1024,1024]{1,0:T(8,128)(2,1)}, u32[]{:S(2)}) copy-start(bf16[1024,1024]{1,0:T(8,128)(2,1)} %constant.8.clone.high_ref) | copy-start | bytes 6291460
  168.7 30.8 %all-to-all-start.5 = ((f32[1024,1,256]{2,1,0:T(1,128)}), f32[1024,1,256]{2,1,0:T(1,128)S(1)}, u32[]{:S(2)}, u32[]{:S(2)}) async-start(f32[1024,1,256]{2,1,0:T(1,128)} %copy.46), calls=%async_computation.5 | async-start | bytes 2097152 | tf_op jit(solution)/shard_map/all_to_all | solution.py:335

commit v2 on v1

--- a/solution.py
+++ b/solution.py
@@ -18,6 +18,9 @@
 NZ = 256
 HALF = 128
 FEW = 4
+GROUP = 16
+BLOCK = 64
+MESH = pl.DeviceIdType.MESH
 
 relaxation = 0.8
 small_floor = 1e-06
@@ -32,9 +35,11 @@
     k = np.arange(NPHI)
     phase = (np.outer(k, k) % NPHI) * (2.0 * math.pi / NPHI)
     table = ((np.cos(phase) + np.sin(phase)) / math.sqrt(NPHI)).astype(np.float32)
+    order = k.reshape(GROUP, GROUP, FEW).transpose(1, 0, 2).reshape(-1)
+    table = table[order]
     high = table.astype(jnp.bfloat16)
     low = (table - high.astype(np.float32)).astype(jnp.bfloat16)
-    return high, low
+    return high, low, np.ascontiguousarray(high.T), np.ascontiguousarray(low.T)
 
 
 def parity_table():
@@ -48,33 +53,6 @@
     high = values.astype(bf16)
     low = (values - high.astype(f32)).astype(bf16)
     return high, low
-
-
-def transform_kernel(high_ref, low_ref, perm_ref, x_ref, o_ref, xh, xl):
-    for piece in range(4):
-        rows = pl.ds(piece * 256, 256)
-        h, l = split(x_ref[rows, :])
-        xh[rows, :] = jnp.dot(h, perm_ref[...], preferred_element_type=f32).astype(bf16)
-        xl[rows, :] = jnp.dot(l, perm_ref[...], preferred_element_type=f32).astype(bf16)
-    for piece in range(4):
-        rows = pl.ds(piece * 256, 256)
-        acc = jnp.dot(high_ref[rows, :], xh[...], preferred_element_type=f32)
-        acc += jnp.dot(high_ref[rows, :], xl[...], preferred_element_type=f32)
-        acc += jnp.dot(low_ref[rows, :], xh[...], preferred_element_type=f32)
-        o_ref[rows, :] = acc
-
-
-def transform(high, low, perm, x):
-    return pl.pallas_call(
-        transform_kernel,
-        out_shape=jax.ShapeDtypeStruct((NPHI, NR), f32),
-        scratch_shapes=[pltpu.VMEM((NPHI, NR), bf16), pltpu.VMEM((NPHI, NR), bf16)],
-        compiler_params=pltpu.CompilerParams(vmem_limit_bytes=32 << 20),
-        cost_estimate=pl.CostEstimate(
-            flops=6 * NPHI * NPHI * NR, bytes_accessed=6 << 20, transcendentals=0
-        ),
-        name="transform",
-    )(high, low, perm, x)
 
 
 def lane_ids(rows=1):
@@ -247,60 +225,244 @@
     return factors
 
 
-def solve_kernel(outer_ref, end_ref, perm_ref, f_ref, o_ref, s_ref, f, base, d, w, va, vb, r, ca, cb, cr, flat):
-    step = pl.program_id(0)
-
-    @pl.when(step == 0)
-    def _():
-        held = jnp.concatenate([outer_ref[...], end_ref[...]], axis=0).astype(f32).astype(bf16)
-        held = jnp.concatenate([held] * 8, axis=0)
-        held = jnp.dot(held, perm_ref[...], preferred_element_type=f32)
-        outer_rows = [held[0:1, :HALF], held[0:1, HALF:]]
-        end_rows = [held[1:2, :HALF], held[1:2, HALF:]]
-        setup_base(base, outer_rows, end_rows)
-        for ref in (va, vb):
-            ref[:, 0:PAD, :] = jnp.zeros((4, PAD, HALF), f32)
-            ref[:, HALF + PAD :, :] = jnp.zeros((4, PAD, HALF), f32)
-        for ref in (ca, cb):
-            ref[0:PAD, :] = jnp.zeros((PAD, HALF), f32)
-            ref[HALF + PAD :, :] = jnp.zeros((PAD, HALF), f32)
-
-    mode = (lax.axis_index("phi") * 16 + lax.axis_index("gz")) * FEW + step
-    for ip in range(2):
-        flat[ip] = f_ref[0, :, ip * HALF : (ip + 1) * HALF]
-    for q in range(4):
-        f[q] = flat[q % 2, pl.ds(q // 2, HALF, stride=2), :]
-
-    def write(q, start, value):
-        flat[q % 2, pl.ds(2 * start + q // 2, CH, stride=2), :] = value
-
-    factors = solve_mode(mode, f, base, d, w, va, vb, r, ca, cb, cr, write)
-    for ip in range(2):
-        o_ref[0, :, ip * HALF : (ip + 1) * HALF] = flat[ip]
-    for cycle in range(VCYC):
-        s_ref[0, cycle : cycle + 1, :] = jnp.broadcast_to(factors[cycle], (1, HALF))
-
-
-def solve(outer, end, perm, own):
+def block(index):
+    return pl.ds(pl.multiple_of(index * BLOCK, BLOCK), BLOCK)
+
+
+def peers(me, action):
+    def step(o, carry):
+        action(lax.rem(me + o, GROUP))
+        return carry
+
+    lax.fori_loop(1, GROUP, step, 0)
+
+
+class Exchange:
+    def __init__(self, axis, src, dst, send, recv):
+        self.axis, self.src, self.dst, self.send, self.recv = axis, src, dst, send, recv
+        self.me = lax.axis_index(axis)
+
+    def copy(self, par, t, slot):
+        return pltpu.make_async_remote_copy(
+            src_ref=self.src.at[par, block(t)],
+            dst_ref=self.dst.at[par, block(slot)],
+            send_sem=self.send.at[par, t],
+            recv_sem=self.recv.at[par, slot],
+            device_id={self.axis: t},
+            device_id_type=MESH,
+        )
+
+    def start(self, par, t):
+        self.copy(par, t, self.me).start()
+
+    def start_all(self, par):
+        peers(self.me, lambda t: self.start(par, t))
+
+    def keep(self, par):
+        self.dst[par, block(self.me), :] = self.src[par, block(self.me), :]
+
+    def wait_recv(self, par):
+        peers(self.me, lambda t: self.copy(par, t, t).wait_recv())
+
+    def wait_send(self, par):
+        peers(self.me, lambda t: self.copy(par, t, self.me).wait_send())
+
+
+def hartley(high, low, src, par, xs, exchange):
+    for piece in range(4):
+        rows = pl.ds(piece * 256, 256)
+        h, l = split(src[par, rows, :])
+        xs[rows, :HALF] = h
+        xs[rows, HALF:] = l
+    me = exchange.me
+
+    def step(n, carry):
+        piece = lax.rem(me // 4 + n, 4)
+        rows = pl.ds(pl.multiple_of(piece * 256, 256), 256)
+        both = jnp.dot(high[rows, :], xs[...], preferred_element_type=f32)
+        rest = jnp.dot(low[rows, :], xs[:, :HALF], preferred_element_type=f32)
+        exchange.src[par, rows, :] = both[:, :HALF] + (both[:, HALF:] + rest)
+        for j in range(4):
+            t = piece * 4 + lax.rem(me + j, 4)
+
+            @pl.when(t != me)
+            def _():
+                exchange.start(par, t)
+
+        return carry
+
+    lax.fori_loop(0, 4, step, 0)
+
+
+def main_kernel(
+    charge_ref, outer_ref, end_ref, perm_ref, fh_ref, fl_ref, bh_ref, bl_ref,
+    w_ref, s_ref,
+    xin, xp, t1, r1, s1, r2, r3, r4, o4, p3, p2, q1, v1, xs,
+    fh, fl, bh, bl,
+    f, base, d, w, va, vb, r, ca, cb, cr, sc_src, sc,
+    in_sem, table_sem, keep_sem, send, recv, sc_send, sc_recv,
+):
+    phi, gz = lax.axis_index("phi"), lax.axis_index("gz")
+    load = pltpu.make_async_copy(charge_ref, xin, in_sem)
+    load.start()
+    tables = [
+        pltpu.make_async_copy(src, dst, table_sem.at[n])
+        for n, (src, dst) in enumerate(((fh_ref, fh), (fl_ref, fl), (bh_ref, bh), (bl_ref, bl)))
+    ]
+    for copy in tables:
+        copy.start()
+    barrier = pltpu.get_barrier_semaphore()
+    for axis, me in (("phi", phi), ("gz", gz)):
+        peers(
+            me,
+            lambda t: pl.semaphore_signal(barrier, inc=1, device_id={axis: t}, device_id_type=MESH),
+        )
+
+    first = Exchange("phi", t1, r1, send.at[0], recv.at[0])
+    second = Exchange("gz", s1, r2, send.at[1], recv.at[1])
+    third = Exchange("phi", r3, r4, send.at[2], recv.at[2])
+    fourth = Exchange("phi", o4, p3, send.at[3], recv.at[3])
+    fifth = Exchange("gz", p2, q1, send.at[4], recv.at[4])
+    sixth = Exchange("phi", v1, w_ref, send.at[5], recv.at[5])
+
+    load.wait()
+    for piece in range(4):
+        rows = pl.ds(piece * 256, 256)
+        h, l = split(xin[piece * 16 : (piece + 1) * 16].reshape(256, NR))
+        value = jnp.dot(h, perm_ref[...], preferred_element_type=f32) + jnp.dot(
+            l, perm_ref[...], preferred_element_type=f32
+        )
+        xp[0, rows, :] = value[:, :HALF]
+        xp[1, rows, :] = value[:, HALF:]
+    for par in range(2):
+        for z in range(GROUP):
+            t1[par, z * BLOCK : (z + 1) * BLOCK, :] = xp[par, pl.ds(z, BLOCK, stride=GROUP), :]
+    pl.semaphore_wait(barrier, 2 * (GROUP - 1))
+
+    first.start_all(0)
+    first.start_all(1)
+    first.keep(0)
+    first.keep(1)
+
+    held = jnp.concatenate([outer_ref[...], end_ref[...]], axis=0).astype(f32).astype(bf16)
+    held = jnp.concatenate([held] * 8, axis=0)
+    held = jnp.dot(held, perm_ref[...], preferred_element_type=f32)
+    setup_base(base, [held[0:1, :HALF], held[0:1, HALF:]], [held[1:2, :HALF], held[1:2, HALF:]])
+    for ref in (va, vb):
+        ref[:, 0:PAD, :] = jnp.zeros((4, PAD, HALF), f32)
+        ref[:, HALF + PAD :, :] = jnp.zeros((4, PAD, HALF), f32)
+    for ref in (ca, cb):
+        ref[0:PAD, :] = jnp.zeros((PAD, HALF), f32)
+        ref[HALF + PAD :, :] = jnp.zeros((PAD, HALF), f32)
+    sc_src[...] = jnp.zeros((8, HALF), f32)
+    for copy in tables:
+        copy.wait()
+
+    for par in range(2):
+        first.wait_recv(par)
+        hartley(fh, fl, r1, par, xs, second)
+        second.keep(par)
+        second.wait_recv(par)
+        for b in range(GROUP):
+            r3[par, pl.ds(b, BLOCK, stride=GROUP), :] = r2[par, b * BLOCK : (b + 1) * BLOCK, :]
+        third.start_all(par)
+        third.keep(par)
+
+    third.wait_recv(0)
+    third.wait_recv(1)
+
+    def solve_step(m, carry):
+        mode = (phi * GROUP + gz) * FEW + m
+        for q in range(4):
+            for b in range(GROUP):
+                f[q, 8 * b : 8 * b + 8, :] = r4[
+                    q % 2, pl.ds((q // 2) * BLOCK + m * GROUP + b, 8, stride=HALF), :
+                ]
+
+        def write(q, start, value):
+            for g in range(CH // 8):
+                b = start // 8 + g
+                o4[q % 2, pl.ds((q // 2) * BLOCK + m * GROUP + b, 8, stride=HALF), :] = value[
+                    8 * g : 8 * g + 8
+                ]
+
+        factors = solve_mode(mode, f, base, d, w, va, vb, r, ca, cb, cr, write)
+        row_ids = lax.broadcasted_iota(jnp.int32, (8, HALF), 0)
+        lanes = lane_ids(8)
+        for cycle in range(VCYC):
+            here = (row_ids == cycle) & (lanes == gz * FEW + m)
+            sc_src[...] = sc_src[...] + jnp.where(here, factors[cycle], 0.0)
+        return carry
+
+    lax.fori_loop(0, FEW, solve_step, 0)
+
+    fourth.start_all(0)
+    fourth.start_all(1)
+    fourth.keep(0)
+    fourth.keep(1)
+
+    def scale_copy(t, slot):
+        return pltpu.make_async_remote_copy(
+            src_ref=sc_src,
+            dst_ref=sc.at[slot],
+            send_sem=sc_send.at[t],
+            recv_sem=sc_recv.at[slot],
+            device_id={"gz": t},
+            device_id_type=MESH,
+        )
+
+    peers(gz, lambda t: scale_copy(t, gz).start())
+    sc[gz] = sc_src[...]
+
+    for par in range(2):
+        fourth.wait_recv(par)
+        for b in range(GROUP):
+            p2[par, b * BLOCK : (b + 1) * BLOCK, :] = p3[par, pl.ds(b, BLOCK, stride=GROUP), :]
+        fifth.start_all(par)
+        fifth.keep(par)
+        fifth.wait_recv(par)
+        hartley(bh, bl, q1, par, xs, sixth)
+        pltpu.make_async_copy(
+            v1.at[par, block(phi)], w_ref.at[par, block(phi)], keep_sem.at[par]
+        ).start()
+
+    peers(gz, lambda t: scale_copy(t, t).wait_recv())
+    total = sc[0]
+    for n in range(1, GROUP):
+        total = total + sc[n]
+    s_ref[...] = total[:VCYC, :BLOCK]
+
+    for exchange in (first, second, third, fourth, fifth):
+        for par in range(2):
+            exchange.wait_send(par)
+    peers(gz, lambda t: scale_copy(t, gz).wait_send())
+    for par in range(2):
+        sixth.wait_recv(par)
+        sixth.wait_send(par)
+        pltpu.make_async_copy(
+            v1.at[par, block(phi)], w_ref.at[par, block(phi)], keep_sem.at[par]
+        ).wait()
+
+
+def run(charge, outer, end, tables):
+    rows = lambda: pltpu.VMEM((2, NPHI, HALF), f32)
     quad = lambda n: pltpu.VMEM((n, HALF, HALF), f32)
+    table = lambda: pltpu.VMEM((NPHI, NPHI), bf16)
+    whole = pl.BlockSpec(memory_space=pltpu.VMEM)
+    away = pl.BlockSpec(memory_space=pl.ANY)
     return pl.pallas_call(
-        solve_kernel,
-        grid=(FEW,),
+        main_kernel,
         out_shape=(
-            jax.ShapeDtypeStruct((FEW, NZ, NR), f32),
-            jax.ShapeDtypeStruct((FEW, 8, HALF), f32),
+            jax.ShapeDtypeStruct((2, NPHI, HALF), f32),
+            jax.ShapeDtypeStruct((VCYC, BLOCK), f32),
         ),
-        in_specs=[
-            pl.BlockSpec((1, NZ), lambda m: (0, 0)),
-            pl.BlockSpec((1, NR), lambda m: (0, 0)),
-            pl.BlockSpec((NR, NR), lambda m: (0, 0)),
-            pl.BlockSpec((1, NZ, NR), lambda m: (m, 0, 0)),
-        ],
-        out_specs=(
-            pl.BlockSpec((1, NZ, NR), lambda m: (m, 0, 0)),
-            pl.BlockSpec((1, 8, HALF), lambda m: (m, 0, 0)),
-        ),
+        in_specs=[away, whole, whole, whole, away, away, away, away],
+        out_specs=(away, whole),
         scratch_shapes=[
+            pltpu.VMEM((BLOCK, GROUP, NR), f32),
+            *[rows() for _ in range(12)],
+            pltpu.VMEM((NPHI, NR), bf16),
+            table(), table(), table(), table(),
             quad(4), quad(5), quad(5), quad(4),
             pltpu.VMEM((4, HALF + 2 * PAD, HALF), f32),
             pltpu.VMEM((4, HALF + 2 * PAD, HALF), f32),
@@ -308,40 +470,72 @@
             pltpu.VMEM((HALF + 2 * PAD, HALF), f32),
             pltpu.VMEM((HALF + 2 * PAD, HALF), f32),
             pltpu.VMEM((HALF, HALF), f32),
-            pltpu.VMEM((2, NZ, HALF), f32),
+            pltpu.VMEM((8, HALF), f32),
+            pltpu.VMEM((GROUP, 8, HALF), f32),
+            pltpu.SemaphoreType.DMA,
+            pltpu.SemaphoreType.DMA((4,)),
+            pltpu.SemaphoreType.DMA((2,)),
+            pltpu.SemaphoreType.DMA((6, 2, GROUP)),
+            pltpu.SemaphoreType.DMA((6, 2, GROUP)),
+            pltpu.SemaphoreType.DMA((GROUP,)),
+            pltpu.SemaphoreType.DMA((GROUP,)),
         ],
-        compiler_params=pltpu.CompilerParams(vmem_limit_bytes=32 << 20),
-        cost_estimate=pl.CostEstimate(
-            flops=200 * FEW * NZ * NR, bytes_accessed=2 << 20, transcendentals=0
+        compiler_params=pltpu.CompilerParams(
+            collective_id=0, has_side_effects=True, vmem_limit_bytes=48 << 20
         ),
-        name="solve",
-    )(outer, end, perm, own)
+        name="modes",
+    )(charge, outer, end, *tables)
+
+
+def finish_kernel(perm_ref, w_ref, o_ref, rows):
+    for z in range(0, GROUP, 4):
+        flat = jnp.concatenate(
+            [w_ref[0, z : z + 4].reshape(4 * GROUP, HALF), w_ref[1, z : z + 4].reshape(4 * GROUP, HALF)],
+            axis=1,
+        )
+        h, l = split(flat)
+        value = jnp.dot(h, perm_ref[...], preferred_element_type=f32) + jnp.dot(
+            l, perm_ref[...], preferred_element_type=f32
+        )
+        for g in range(4):
+            for half in range(2):
+                rows[half, pl.ds(z + g, GROUP, stride=GROUP), :] = value[
+                    g * GROUP : (g + 1) * GROUP, half * HALF : (half + 1) * HALF
+                ]
+    for half in range(2):
+        o_ref[:, :, half * HALF : (half + 1) * HALF] = rows[half].reshape(GROUP, GROUP, HALF)
+
+
+def finish(perm, w):
+    return pl.pallas_call(
+        finish_kernel,
+        grid=(4,),
+        out_shape=jax.ShapeDtypeStruct((BLOCK, GROUP, NR), f32),
+        in_specs=[
+            pl.BlockSpec((NR, NR), lambda n: (0, 0)),
+            pl.BlockSpec((2, GROUP, GROUP, HALF), lambda n: (0, 0, n, 0)),
+        ],
+        out_specs=pl.BlockSpec((GROUP, GROUP, NR), lambda n: (n, 0, 0)),
+        scratch_shapes=[pltpu.VMEM((2, GROUP * GROUP, HALF), f32)],
+        compiler_params=pltpu.CompilerParams(vmem_limit_bytes=16 << 20),
+        name="finish",
+    )(perm, w)
 
 
 def body(tables, charge, outer_held, end_held):
-    high, low, forward, backward = (jnp.asarray(t) for t in tables)
-    rows = lax.all_to_all(charge, "phi", split_axis=1, concat_axis=0, tiled=True)
-    spectrum = transform(high, low, forward, rows.reshape(NPHI, NR)).reshape(NPHI, 1, NR)
-    spectrum = lax.all_to_all(spectrum, "phi", split_axis=0, concat_axis=1, tiled=True)
-    own = lax.all_to_all(spectrum, "gz", split_axis=0, concat_axis=1, tiled=True)
+    forward, backward, *hartleys = (jnp.asarray(t) for t in tables)
     outer = outer_held.reshape(1, NZ)
     end = end_held.reshape(1, NR)
-    local, scale_rows = solve(outer, end, forward, own)
-    mine = jnp.transpose(scale_rows[:, :VCYC, 0])
-    scales = lax.all_gather(mine, "gz", axis=1, tiled=True)
-    back = lax.all_to_all(local, "gz", split_axis=1, concat_axis=0, tiled=True)
-    back = lax.all_to_all(back, "phi", split_axis=1, concat_axis=0, tiled=True)
-    rows_back = transform(high, low, backward, back.reshape(NPHI, NR)).reshape(NPHI, 1, NR)
-    potential = lax.all_to_all(rows_back, "phi", split_axis=0, concat_axis=1, tiled=True)
+    w, scales = run(charge, outer, end, (forward, *hartleys))
+    potential = finish(backward, w.reshape(2, GROUP, BLOCK, HALF))
     return (potential, scales)
 
 
 def solution(mesh):
     in_specs = (P("phi", "gz", None), P(), P())
     out_specs = (P("phi", "gz", None), P(None, "phi"))
-    high, low = hartley_tables()
     perm = parity_table()
-    tables = (high, low, perm, np.ascontiguousarray(perm.T))
+    tables = (perm, np.ascontiguousarray(perm.T), *hartley_tables())
     return jax.shard_map(
         functools.partial(body, tables), mesh=mesh, in_specs=in_specs, out_specs=out_specs, check_vma=False
     )

time: 202 us -> 135 us (0.67)
  blocking collectives: 164 us -> 0 us
  Pallas kernels: 12.6 us -> 129 us
  waiting for transfers between devices: 9.17 us -> 0 us
  local copies, waits for them, and re-layouts: 11.4 us -> 5.64 us
  starting transfers between devices: 3.55 us -> 0 us
    all_to_all x5 -> x0, blocking collectives: 146 us -> none  [the longest x1 38.3 us: body(): lax.all_to_all(charge, 'phi', split_axis=1, concat_axis=0, tiled=True)]
    pallas_call x3 -> x2, Pallas kernels: 12.6 us -> 129 us  [the longest x1 126 us: run(): pl.pallas_call(main_kernel, out_shape=(jax.ShapeDtypeStruct((2, NPHI, HAL...]
    all_gather x1 -> x0, blocking collectives: 17.3 us -> none  [body(): scales = lax.all_gather(mine, 'gz', axis=1, tiled=True)]
    all_to_all x1 -> x0, waiting for transfers between devices: 9.17 us -> none  [body(): lax.all_to_all(rows_back, 'phi', split_axis=0, concat_axis=1, tiled=True)]
    all_to_all x5 -> x0, local copies, waits for them, and re-layouts: 3.87 us -> none  [the longest x2 1.6 us: body(): back = lax.all_to_all(local, 'gz', split_axis=1, concat_axis=0, tiled=True)]
    all_to_all x1 -> x0, starting transfers between devices: 3.55 us -> none  [body(): lax.all_to_all(rows_back, 'phi', split_axis=0, concat_axis=1, tiled=True)]
    reshape x2 -> x0, local copies, waits for them, and re-layouts: 3.13 us -> none  [the longest x1 2.05 us: body(): transform(high, low, backward, back.reshape(NPHI, NR)).reshape(NPHI, 1, NR)]
    unnamed x17 -> x13, local copies, waits for them, and re-layouts: 3.65 us -> 5.64 us
  transfers between devices with their start and end apart: 1 -> 0, of which waited for: 1 -> 0; matrix products, arithmetic and copies ran while one was open for 0% -> 0% of each run, Pallas kernels for 0% -> 0%
where the time goes in v2:
time: 135 us
  Pallas kernels  129 us (96%)
  local copies, waits for them, and re-layouts  5.64 us (4%)
    pallas_call x1, Pallas kernels, run(): pl.pallas_call(main_kernel, out_shape=(jax.ShapeDtypeStruct((2, NPHI, HAL...  126 us
    unnamed x13, local copies, waits for them, and re-layouts  5.64 us

profile of v2, /device:TPU:1, one launch (start us, length us, event | category | flops | bytes accessed | tf_op | source)
XLA Modules:
  0.0 135.3 jit_solution(15747254657481494349)
XLA Ops:
  0.6 0.0 copy-start
  0.6 1.6 %copy-done = bf16[1024,1024]{1,0:T(8,128)(2,1)S(1)} copy-done((bf16[1024,1024]{1,0:T(8,128)(2,1)S(1)}, bf16[1024,1024]{1,0:T(8,128)(2,1)}, u32[]{:S(2)}) %copy-start) | copy-done | bytes 2097176
  2.2 0.0 copy-start.1
  2.2 1.2 copy-done.1
  3.5 0.0 copy-start.3
  3.5 0.9 copy-done.3
  4.4 0.0 copy-start.4
  4.4 0.7 copy-done.4
  5.0 0.0 copy-start.5
  5.0 0.7 copy-done.5
  5.7 0.0 copy-start.2
  5.7 126.5 %modes.1 = (f32[2,1024,128]{2,1,0:T(8,128)S(1)}, f32[2,64]{1,0:T(2,128)S(1)}) custom-call(f32[64,16,256]{2,1,0:T(8,128)S(1)} %copy-done.1, s32[1,256]{1,0:T(1,128)S(1)} %bitcast.4, s32[1,256]{1,0:T(1,128)S(1)} %bitcast.5, bf16[256,256]{1,0:T(8,128)(2,1)S(1)} %copy-done.3, bf16[1024,1024]{1,0:T(8,128)(2,1)S(1)} %copy-done, ...), custom_call_target="tpu_custom_call" | custom-call | tf_op jit(solution)/shard_map/modes/pallas_call | solution.py:453
  132.2 0.0 copy-done.2
  132.2 2.5 %finish.1 = f32[64,16,256]{2,1,0:T(8,128)} custom-call(bf16[256,256]{1,0:T(8,128)(2,1)S(1)} %copy-done.2, f32[2,16,64,128]{3,2,1,0:T(8,128)S(1)} %bitcast.3), custom_call_target="tpu_custom_call" | custom-call | tf_op jit(solution)/shard_map/finish/pallas_call | solution.py:510
  134.7 0.6 copy.12
Async XLA Ops:
  0.6 1.6 %copy-start = (bf16[1024,1024]{1,0:T(8,128)(2,1)S(1)}, bf16[1024,1024]{1,0:T(8,128)(2,1)}, u32[]{:S(2)}) copy-start(bf16[1024,1024]{1,0:T(8,128)(2,1)} %constant.14.clone.fh_ref) | copy-start | bytes 6291460
  2.2 1.2 copy-start.1
  3.5 0.9 copy-start.3
  4.4 0.7 copy-start.4
  5.0 0.7 copy-start.5
  5.7 126.5 %copy-start.2 = (bf16[256,256]{1,0:T(8,128)(2,1)S(1)}, bf16[256,256]{1,0:T(8,128)(2,1)}, u32[]{:S(2)}) copy-start(bf16[256,256]{1,0:T(8,128)(2,1)} %constant.13.clone.perm_ref) | copy-start | bytes 393220

commit v3 on v2

--- a/solution.py
+++ b/solution.py
@@ -242,30 +242,41 @@
         self.axis, self.src, self.dst, self.send, self.recv = axis, src, dst, send, recv
         self.me = lax.axis_index(axis)
 
-    def copy(self, par, t, slot):
+    def copy(self, par, source, target, t, sem):
         return pltpu.make_async_remote_copy(
-            src_ref=self.src.at[par, block(t)],
-            dst_ref=self.dst.at[par, block(slot)],
-            send_sem=self.send.at[par, t],
-            recv_sem=self.recv.at[par, slot],
+            src_ref=self.src.at[par, source],
+            dst_ref=self.dst.at[par, target],
+            send_sem=self.send.at[par],
+            recv_sem=self.recv.at[sem],
             device_id={self.axis: t},
             device_id_type=MESH,
         )
 
     def start(self, par, t):
-        self.copy(par, t, self.me).start()
+        self.copy(par, block(t), block(self.me), t, par).start()
 
     def start_all(self, par):
         peers(self.me, lambda t: self.start(par, t))
 
+    def start_mode(self, par, m, sem):
+        rows = lambda n: pl.ds(pl.multiple_of(n * BLOCK + m * GROUP, GROUP), GROUP)
+        peers(self.me, lambda t: self.copy(par, rows(t), rows(self.me), t, sem).start())
+
     def keep(self, par):
         self.dst[par, block(self.me), :] = self.src[par, block(self.me), :]
 
+    def whole(self, par, rows, sem):
+        t = lax.rem(self.me + 1, GROUP)
+        return self.copy(par, pl.ds(0, rows), pl.ds(0, rows), t, sem)
+
     def wait_recv(self, par):
-        peers(self.me, lambda t: self.copy(par, t, t).wait_recv())
+        self.whole(par, (GROUP - 1) * BLOCK, par).wait_recv()
+
+    def wait_recv_mode(self, par, sem):
+        self.whole(par, (GROUP - 1) * GROUP, sem).wait_recv()
 
     def wait_send(self, par):
-        peers(self.me, lambda t: self.copy(par, t, self.me).wait_send())
+        self.whole(par, (GROUP - 1) * BLOCK, par).wait_send()
 
 
 def hartley(high, low, src, par, xs, exchange):
@@ -365,13 +376,17 @@
         second.wait_recv(par)
         for b in range(GROUP):
             r3[par, pl.ds(b, BLOCK, stride=GROUP), :] = r2[par, b * BLOCK : (b + 1) * BLOCK, :]
-        third.start_all(par)
+        if par == 0:
+            third.start_all(par)
+        else:
+            for m in range(FEW):
+                third.start_mode(par, m, 1 + m)
         third.keep(par)
 
     third.wait_recv(0)
-    third.wait_recv(1)
 
     def solve_step(m, carry):
+        third.wait_recv_mode(1, 1 + m)
         mode = (phi * GROUP + gz) * FEW + m
         for q in range(4):
             for b in range(GROUP):
@@ -392,26 +407,26 @@
         for cycle in range(VCYC):
             here = (row_ids == cycle) & (lanes == gz * FEW + m)
             sc_src[...] = sc_src[...] + jnp.where(here, factors[cycle], 0.0)
+        fourth.start_mode(0, m, 0)
         return carry
 
     lax.fori_loop(0, FEW, solve_step, 0)
 
-    fourth.start_all(0)
     fourth.start_all(1)
     fourth.keep(0)
     fourth.keep(1)
 
-    def scale_copy(t, slot):
+    def scale_copy(source, target, t):
         return pltpu.make_async_remote_copy(
-            src_ref=sc_src,
-            dst_ref=sc.at[slot],
-            send_sem=sc_send.at[t],
-            recv_sem=sc_recv.at[slot],
+            src_ref=source,
+            dst_ref=target,
+            send_sem=sc_send,
+            recv_sem=sc_recv,
             device_id={"gz": t},
             device_id_type=MESH,
         )
 
-    peers(gz, lambda t: scale_copy(t, gz).start())
+    peers(gz, lambda t: scale_copy(sc_src, sc.at[gz], t).start())
     sc[gz] = sc_src[...]
 
     for par in range(2):
@@ -426,7 +441,9 @@
             v1.at[par, block(phi)], w_ref.at[par, block(phi)], keep_sem.at[par]
         ).start()
 
-    peers(gz, lambda t: scale_copy(t, t).wait_recv())
+    others = sc.at[pl.ds(0, GROUP - 1)]
+    all_scales = scale_copy(others, others, lax.rem(gz + 1, GROUP))
+    all_scales.wait_recv()
     total = sc[0]
     for n in range(1, GROUP):
         total = total + sc[n]
@@ -435,7 +452,7 @@
     for exchange in (first, second, third, fourth, fifth):
         for par in range(2):
             exchange.wait_send(par)
-    peers(gz, lambda t: scale_copy(t, gz).wait_send())
+    all_scales.wait_send()
     for par in range(2):
         sixth.wait_recv(par)
         sixth.wait_send(par)
@@ -475,13 +492,13 @@
             pltpu.SemaphoreType.DMA,
             pltpu.SemaphoreType.DMA((4,)),
             pltpu.SemaphoreType.DMA((2,)),
-            pltpu.SemaphoreType.DMA((6, 2, GROUP)),
-            pltpu.SemaphoreType.DMA((6, 2, GROUP)),
-            pltpu.SemaphoreType.DMA((GROUP,)),
-            pltpu.SemaphoreType.DMA((GROUP,)),
+            pltpu.SemaphoreType.DMA((6, 2)),
+            pltpu.SemaphoreType.DMA((6, 5)),
+            pltpu.SemaphoreType.DMA,
+            pltpu.SemaphoreType.DMA,
         ],
         compiler_params=pltpu.CompilerParams(
-            collective_id=0, has_side_effects=True, vmem_limit_bytes=48 << 20
+            collective_id=0, has_side_effects=True, vmem_limit_bytes=62 << 20
         ),
         name="modes",
     )(charge, outer, end, *tables)

time: 135 us -> 118 us (0.87)
  Pallas kernels: 129 us -> 115 us
  local copies, waits for them, and re-layouts: 5.64 us -> 1.79 us
    pallas_call x1, Pallas kernels: 126 us -> 113 us  [run(): pl.pallas_call(main_kernel, out_shape=(jax.ShapeDtypeStruct((2, NPHI, HAL...]
    unnamed x13 -> x7, local copies, waits for them, and re-layouts: 5.64 us -> 1.79 us
where the time goes in v3:
time: 118 us
  Pallas kernels  115 us (97%)
  local copies, waits for them, and re-layouts  1.79 us (2%)
    pallas_call x1, Pallas kernels, run(): pl.pallas_call(main_kernel, out_shape=(jax.ShapeDtypeStruct((2, NPHI, HAL...  113 us
    pallas_call x1, Pallas kernels, finish(): pl.pallas_call(finish_kernel, grid=(4,), out_shape=jax.ShapeDtypeStruct((...  2.49 us

profile of v3, /device:TPU:1, one launch (start us, length us, event | category | flops | bytes accessed | tf_op | source)
XLA Modules:
  0.0 117.6 jit_solution(15128128632771507523)
XLA Ops:
  0.6 0.0 copy-start.1
  0.6 112.7 %modes.1 = (f32[2,1024,128]{2,1,0:T(8,128)}, f32[2,64]{1,0:T(2,128)}) custom-call(f32[64,16,256]{2,1,0:T(8,128)} %charge_ref.1, s32[1,256]{1,0:T(1,128)} %bitcast.4, s32[1,256]{1,0:T(1,128)} %bitcast.5, bf16[256,256]{1,0:T(8,128)(2,1)} %constant.12.clone.perm_ref, bf16[1024,1024]{1,0:T(8,128)(2,1)} %constant.14.clone.fh_ref, ...), custom_call_target="tpu_custom_call" | custom-call | tf_op jit(solution)/shard_map/modes/pallas_call | solution.py:470
  113.3 0.0 copy-start.2
  113.3 0.0 copy-done.1
  113.3 0.0 copy-start
  113.3 1.2 %copy-done = f32[2,1024,128]{2,1,0:T(8,128)S(1)} copy-done((f32[2,1024,128]{2,1,0:T(8,128)S(1)}, f32[2,1024,128]{2,1,0:T(8,128)}, u32[]{:S(2)}) %copy-start) | copy-done | bytes 1048600
  114.5 2.5 %finish.1 = f32[64,16,256]{2,1,0:T(8,128)} custom-call(bf16[256,256]{1,0:T(8,128)(2,1)S(1)} %copy-done.1, f32[2,16,64,128]{3,2,1,0:T(8,128)S(1)} %bitcast.3), custom_call_target="tpu_custom_call" | custom-call | tf_op jit(solution)/shard_map/finish/pallas_call | solution.py:527
  117.0 0.0 copy-done.2
  117.0 0.6 copy.12
Async XLA Ops:
  0.6 112.7 %copy-start.1 = (bf16[256,256]{1,0:T(8,128)(2,1)S(1)}, bf16[256,256]{1,0:T(8,128)(2,1)}, u32[]{:S(2)}) copy-start(bf16[256,256]{1,0:T(8,128)(2,1)} %constant.13.clone.perm_ref) | copy-start | bytes 393220
  113.3 3.7 %copy-start.2 = (f32[2,64]{1,0:T(2,128)S(1)}, f32[2,64]{1,0:T(2,128)}, u32[]{:S(2)}) copy-start(f32[2,64]{1,0:T(2,128)} %get-tuple-element.9) | copy-start | bytes 1540
  113.3 1.2 %copy-start = (f32[2,1024,128]{2,1,0:T(8,128)S(1)}, f32[2,1024,128]{2,1,0:T(8,128)}, u32[]{:S(2)}) copy-start(f32[2,1024,128]{2,1,0:T(8,128)} %get-tuple-element.4) | copy-start | bytes 3145732

commit v4 on v3

--- a/solution.py
+++ b/solution.py
@@ -35,18 +35,11 @@
     k = np.arange(NPHI)
     phase = (np.outer(k, k) % NPHI) * (2.0 * math.pi / NPHI)
     table = ((np.cos(phase) + np.sin(phase)) / math.sqrt(NPHI)).astype(np.float32)
-    order = k.reshape(GROUP, GROUP, FEW).transpose(1, 0, 2).reshape(-1)
+    order = k.reshape(GROUP, GROUP, FEW).transpose(1, 2, 0).reshape(-1)
     table = table[order]
     high = table.astype(jnp.bfloat16)
     low = (table - high.astype(np.float32)).astype(jnp.bfloat16)
     return high, low, np.ascontiguousarray(high.T), np.ascontiguousarray(low.T)
-
-
-def parity_table():
-    perm = np.zeros((NR, NR), np.float32)
-    i = np.arange(NR)
-    perm[i, (i % 2) * HALF + i // 2] = 1.0
-    return perm.astype(jnp.bfloat16)
 
 
 def split(values):
@@ -101,6 +94,27 @@
     value = value - jnp.where(j == HALF - 1, outward * open_outer, 0.0)
     value = value - jnp.where((y == 0) | (y == HALF - 1), 0.25 * open_end, 0.0)
     base_ref[4] = value
+
+
+def parity_matrix(half):
+    cell = lax.broadcasted_iota(jnp.int32, (HALF, HALF), 0)
+    lane = lax.broadcasted_iota(jnp.int32, (HALF, HALF), 1)
+    second = (cell % 2) != half
+    target = cell // 2 + jnp.where(second, HALF // 2, 0)
+    return jnp.where(lane == target, 1.0, 0.0)
+
+
+def even_odd(first, second):
+    low = lane_ids(first.shape[0]) < HALF // 2
+    even = jnp.where(low, first, second)
+    odd = pltpu.roll(jnp.where(low, second, first), HALF // 2, 1)
+    return even, odd
+
+
+def two_halves(even, odd):
+    low = lane_ids(even.shape[0]) < HALF // 2
+    odd = pltpu.roll(odd, HALF // 2, 1)
+    return jnp.where(low, even, odd), jnp.where(low, odd, even)
 
 
 def left_of(value):
@@ -147,14 +161,16 @@
     def sweep(src, dst, emit=None):
         for c in range(count):
             centre, near = neighbours(src, c)
+            values = []
             for q in range(4):
                 value = (1.0 - relaxation) * centre[q] + w_ref[q, chunks[c], :] * (
                     f_ref[q, chunks[c], :] + near[q]
                 )
                 if emit is None:
                     dst[q, padded[c], :] = value
-                else:
-                    emit(q, c * CH, value)
+                values.append(value)
+            if emit is not None:
+                emit(c * CH, values)
 
     for c in range(count):
         for q in range(4):
@@ -230,16 +246,18 @@
 
 
 def peers(me, action):
-    def step(o, carry):
-        action(lax.rem(me + o, GROUP))
+    def step(n, carry):
+        away = (n // 2 + 1) * (1 - 2 * lax.rem(n, 2))
+        action(lax.rem(me + GROUP + away, GROUP))
         return carry
 
-    lax.fori_loop(1, GROUP, step, 0)
+    lax.fori_loop(0, GROUP - 1, step, 0)
 
 
 class Exchange:
-    def __init__(self, axis, src, dst, send, recv):
+    def __init__(self, axis, src, dst, send, recv, base):
         self.axis, self.src, self.dst, self.send, self.recv = axis, src, dst, send, recv
+        self.base = base
         self.me = lax.axis_index(axis)
 
     def copy(self, par, source, target, t, sem):
@@ -247,7 +265,7 @@
             src_ref=self.src.at[par, source],
             dst_ref=self.dst.at[par, target],
             send_sem=self.send.at[par],
-            recv_sem=self.recv.at[sem],
+            recv_sem=self.recv.at[self.base + sem],
             device_id={self.axis: t},
             device_id_type=MESH,
         )
@@ -279,12 +297,12 @@
         self.whole(par, (GROUP - 1) * BLOCK, par).wait_send()
 
 
-def hartley(high, low, src, par, xs, exchange):
+def hartley(high, low, src, par, order, xs, exchange):
     for piece in range(4):
         rows = pl.ds(piece * 256, 256)
         h, l = split(src[par, rows, :])
-        xs[rows, :HALF] = h
-        xs[rows, HALF:] = l
+        xs[rows, :HALF] = jnp.dot(h, order, preferred_element_type=f32).astype(bf16)
+        xs[rows, HALF:] = jnp.dot(l, order, preferred_element_type=f32).astype(bf16)
     me = exchange.me
 
     def step(n, carry):
@@ -306,19 +324,23 @@
 
 
 def main_kernel(
-    charge_ref, outer_ref, end_ref, perm_ref, fh_ref, fl_ref, bh_ref, bl_ref,
+    charge_ref, outer_ref, end_ref, fh_ref, fl_ref, bh_ref, bl_ref,
     w_ref, s_ref,
-    xin, xp, t1, r1, s1, r2, r3, r4, o4, p3, p2, q1, v1, xs,
+    outer, end, xin, t1, r1, s1, r2, r3, r4, o4, p3, p2, q1, v1, order, xs,
     fh, fl, bh, bl,
     f, base, d, w, va, vb, r, ca, cb, cr, sc_src, sc,
-    in_sem, table_sem, keep_sem, send, recv, sc_send, sc_recv,
+    in_sem, table_sem, send, recv, sc_send, sc_recv,
 ):
     phi, gz = lax.axis_index("phi"), lax.axis_index("gz")
-    load = pltpu.make_async_copy(charge_ref, xin, in_sem)
-    load.start()
+    loads = [
+        pltpu.make_async_copy(charge_ref.at[:, pl.ds(half * HALF, HALF)], xin.at[half], in_sem.at[half])
+        for half in range(2)
+    ]
+    for copy in loads:
+        copy.start()
     tables = [
         pltpu.make_async_copy(src, dst, table_sem.at[n])
-        for n, (src, dst) in enumerate(((fh_ref, fh), (fl_ref, fl), (bh_ref, bh), (bl_ref, bl)))
+        for n, (src, dst) in enumerate(((outer_ref, outer), (end_ref, end), (fh_ref, fh), (fl_ref, fl), (bh_ref, bh), (bl_ref, bl)))
     ]
     for copy in tables:
         copy.start()
@@ -329,36 +351,41 @@
             lambda t: pl.semaphore_signal(barrier, inc=1, device_id={axis: t}, device_id_type=MESH),
         )
 
-    first = Exchange("phi", t1, r1, send.at[0], recv.at[0])
-    second = Exchange("gz", s1, r2, send.at[1], recv.at[1])
-    third = Exchange("phi", r3, r4, send.at[2], recv.at[2])
-    fourth = Exchange("phi", o4, p3, send.at[3], recv.at[3])
-    fifth = Exchange("gz", p2, q1, send.at[4], recv.at[4])
-    sixth = Exchange("phi", v1, w_ref, send.at[5], recv.at[5])
-
-    load.wait()
-    for piece in range(4):
-        rows = pl.ds(piece * 256, 256)
-        h, l = split(xin[piece * 16 : (piece + 1) * 16].reshape(256, NR))
-        value = jnp.dot(h, perm_ref[...], preferred_element_type=f32) + jnp.dot(
-            l, perm_ref[...], preferred_element_type=f32
+    first = Exchange("phi", t1, r1, send.at[0], recv, 0)
+    second = Exchange("gz", s1, r2, send.at[1], recv, 2)
+    third = Exchange("phi", r3, r4, send.at[2], recv, 4)
+    fourth = Exchange("phi", o4, p3, send.at[3], recv, 9)
+    fifth = Exchange("gz", p2, q1, send.at[4], recv, 17)
+    sixth = Exchange("phi", v1, w_ref, send.at[5], recv, 19)
+
+    for half in range(2):
+        loads[half].wait()
+        if half == 0:
+            pl.semaphore_wait(barrier, 2 * (GROUP - 1))
+
+        def regroup(t):
+            t1[half, block(t), :] = xin[half, pl.ds(t, BLOCK, stride=GROUP), :]
+            first.start(half, t)
+
+        peers(phi, regroup)
+        r1[half, block(phi), :] = xin[half, pl.ds(phi, BLOCK, stride=GROUP), :]
+
+    for copy in tables:
+        copy.wait()
+    orders = [parity_matrix(0), parity_matrix(1)]
+    held = jnp.concatenate([outer[...]] * 4 + [end[...]] * 4, axis=0).astype(f32)
+    held = even_odd(*(
+        jnp.dot(
+            held[:, n * HALF : (n + 1) * HALF].astype(bf16),
+            orders[n].astype(bf16),
+            preferred_element_type=f32,
         )
-        xp[0, rows, :] = value[:, :HALF]
-        xp[1, rows, :] = value[:, HALF:]
-    for par in range(2):
-        for z in range(GROUP):
-            t1[par, z * BLOCK : (z + 1) * BLOCK, :] = xp[par, pl.ds(z, BLOCK, stride=GROUP), :]
-    pl.semaphore_wait(barrier, 2 * (GROUP - 1))
-
-    first.start_all(0)
-    first.start_all(1)
-    first.keep(0)
-    first.keep(1)
-
-    held = jnp.concatenate([outer_ref[...], end_ref[...]], axis=0).astype(f32).astype(bf16)
-    held = jnp.concatenate([held] * 8, axis=0)
-    held = jnp.dot(held, perm_ref[...], preferred_element_type=f32)
-    setup_base(base, [held[0:1, :HALF], held[0:1, HALF:]], [held[1:2, :HALF], held[1:2, HALF:]])
+        for n in range(2)
+    ))
+    setup_base(base, [row[0:1] for row in held], [row[4:5] for row in held])
+    for n in range(2):
+        order[n] = orders[n].astype(bf16)
+        order[2 + n] = jnp.transpose(orders[n]).astype(bf16)
     for ref in (va, vb):
         ref[:, 0:PAD, :] = jnp.zeros((4, PAD, HALF), f32)
         ref[:, HALF + PAD :, :] = jnp.zeros((4, PAD, HALF), f32)
@@ -366,16 +393,17 @@
         ref[0:PAD, :] = jnp.zeros((PAD, HALF), f32)
         ref[HALF + PAD :, :] = jnp.zeros((PAD, HALF), f32)
     sc_src[...] = jnp.zeros((8, HALF), f32)
-    for copy in tables:
-        copy.wait()
 
     for par in range(2):
         first.wait_recv(par)
-        hartley(fh, fl, r1, par, xs, second)
+        hartley(fh, fl, r1, par, order[par], xs, second)
         second.keep(par)
         second.wait_recv(par)
         for b in range(GROUP):
-            r3[par, pl.ds(b, BLOCK, stride=GROUP), :] = r2[par, b * BLOCK : (b + 1) * BLOCK, :]
+            for m in range(FEW):
+                r3[par, pl.ds(m * GROUP + b, GROUP, stride=BLOCK), :] = r2[
+                    par, b * BLOCK + m * GROUP : b * BLOCK + (m + 1) * GROUP, :
+                ]
         if par == 0:
             third.start_all(par)
         else:
@@ -388,18 +416,19 @@
     def solve_step(m, carry):
         third.wait_recv_mode(1, 1 + m)
         mode = (phi * GROUP + gz) * FEW + m
-        for q in range(4):
+        rows = lambda zp, b: pl.ds(zp * BLOCK + m * GROUP + b, 8, stride=HALF)
+        for zp in range(2):
             for b in range(GROUP):
-                f[q, 8 * b : 8 * b + 8, :] = r4[
-                    q % 2, pl.ds((q // 2) * BLOCK + m * GROUP + b, 8, stride=HALF), :
-                ]
-
-        def write(q, start, value):
-            for g in range(CH // 8):
-                b = start // 8 + g
-                o4[q % 2, pl.ds((q // 2) * BLOCK + m * GROUP + b, 8, stride=HALF), :] = value[
-                    8 * g : 8 * g + 8
-                ]
+                even, odd = even_odd(r4[0, rows(zp, b), :], r4[1, rows(zp, b), :])
+                f[2 * zp, 8 * b : 8 * b + 8, :] = even
+                f[2 * zp + 1, 8 * b : 8 * b + 8, :] = odd
+
+        def write(start, values):
+            for zp in range(2):
+                halves = two_halves(values[2 * zp], values[2 * zp + 1])
+                for g in range(CH // 8):
+                    for n in range(2):
+                        o4[n, rows(zp, start // 8 + g), :] = halves[n][8 * g : 8 * g + 8]
 
         factors = solve_mode(mode, f, base, d, w, va, vb, r, ca, cb, cr, write)
         row_ids = lax.broadcasted_iota(jnp.int32, (8, HALF), 0)
@@ -407,12 +436,13 @@
         for cycle in range(VCYC):
             here = (row_ids == cycle) & (lanes == gz * FEW + m)
             sc_src[...] = sc_src[...] + jnp.where(here, factors[cycle], 0.0)
-        fourth.start_mode(0, m, 0)
+        fourth.start_mode(0, m, m)
         return carry
 
     lax.fori_loop(0, FEW, solve_step, 0)
 
-    fourth.start_all(1)
+    for m in range(FEW):
+        fourth.start_mode(1, m, FEW + m)
     fourth.keep(0)
     fourth.keep(1)
 
@@ -430,16 +460,17 @@
     sc[gz] = sc_src[...]
 
     for par in range(2):
-        fourth.wait_recv(par)
-        for b in range(GROUP):
-            p2[par, b * BLOCK : (b + 1) * BLOCK, :] = p3[par, pl.ds(b, BLOCK, stride=GROUP), :]
-        fifth.start_all(par)
+        for m in range(FEW):
+            fourth.wait_recv_mode(par, par * FEW + m)
+            for b in range(GROUP):
+                p2[par, b * BLOCK + m * GROUP : b * BLOCK + (m + 1) * GROUP, :] = p3[
+                    par, pl.ds(m * GROUP + b, GROUP, stride=BLOCK), :
+                ]
+            fifth.start_mode(par, m, par)
         fifth.keep(par)
         fifth.wait_recv(par)
-        hartley(bh, bl, q1, par, xs, sixth)
-        pltpu.make_async_copy(
-            v1.at[par, block(phi)], w_ref.at[par, block(phi)], keep_sem.at[par]
-        ).start()
+        hartley(bh, bl, q1, par, order[2 + par], xs, sixth)
+        sixth.keep(par)
 
     others = sc.at[pl.ds(0, GROUP - 1)]
     all_scales = scale_copy(others, others, lax.rem(gz + 1, GROUP))
@@ -456,9 +487,6 @@
     for par in range(2):
         sixth.wait_recv(par)
         sixth.wait_send(par)
-        pltpu.make_async_copy(
-            v1.at[par, block(phi)], w_ref.at[par, block(phi)], keep_sem.at[par]
-        ).wait()
 
 
 def run(charge, outer, end, tables):
@@ -473,11 +501,13 @@
             jax.ShapeDtypeStruct((2, NPHI, HALF), f32),
             jax.ShapeDtypeStruct((VCYC, BLOCK), f32),
         ),
-        in_specs=[away, whole, whole, whole, away, away, away, away],
-        out_specs=(away, whole),
+        in_specs=[away] * 7,
+        out_specs=(whole, whole),
         scratch_shapes=[
-            pltpu.VMEM((BLOCK, GROUP, NR), f32),
+            pltpu.VMEM((1, NZ), jnp.int32),
+            pltpu.VMEM((1, NR), jnp.int32),
             *[rows() for _ in range(12)],
+            pltpu.VMEM((4, HALF, HALF), bf16),
             pltpu.VMEM((NPHI, NR), bf16),
             table(), table(), table(), table(),
             quad(4), quad(5), quad(5), quad(4),
@@ -489,11 +519,10 @@
             pltpu.VMEM((HALF, HALF), f32),
             pltpu.VMEM((8, HALF), f32),
             pltpu.VMEM((GROUP, 8, HALF), f32),
-            pltpu.SemaphoreType.DMA,
-            pltpu.SemaphoreType.DMA((4,)),
             pltpu.SemaphoreType.DMA((2,)),
+            pltpu.SemaphoreType.DMA((6,)),
             pltpu.SemaphoreType.DMA((6, 2)),
-            pltpu.SemaphoreType.DMA((6, 5)),
+            pltpu.SemaphoreType.DMA((21,)),
             pltpu.SemaphoreType.DMA,
             pltpu.SemaphoreType.DMA,
         ],
@@ -504,55 +533,54 @@
     )(charge, outer, end, *tables)
 
 
-def finish_kernel(perm_ref, w_ref, o_ref, rows):
-    for z in range(0, GROUP, 4):
-        flat = jnp.concatenate(
-            [w_ref[0, z : z + 4].reshape(4 * GROUP, HALF), w_ref[1, z : z + 4].reshape(4 * GROUP, HALF)],
-            axis=1,
-        )
-        h, l = split(flat)
-        value = jnp.dot(h, perm_ref[...], preferred_element_type=f32) + jnp.dot(
-            l, perm_ref[...], preferred_element_type=f32
-        )
-        for g in range(4):
-            for half in range(2):
-                rows[half, pl.ds(z + g, GROUP, stride=GROUP), :] = value[
-                    g * GROUP : (g + 1) * GROUP, half * HALF : (half + 1) * HALF
-                ]
+def finish_kernel(w_ref, o_ref, rows, out, load_sem, store_sem):
+    loads = [pltpu.make_async_copy(w_ref.at[half], rows.at[half], load_sem.at[half]) for half in range(2)]
+    stores = [
+        pltpu.make_async_copy(out.at[half], o_ref.at[:, :, pl.ds(half * HALF, HALF)], store_sem.at[half])
+        for half in range(2)
+    ]
     for half in range(2):
-        o_ref[:, :, half * HALF : (half + 1) * HALF] = rows[half].reshape(GROUP, GROUP, HALF)
-
-
-def finish(perm, w):
+        loads[half].start()
+    for half in range(2):
+        loads[half].wait()
+        for q in range(BLOCK):
+            out[half, q] = rows[half, pl.ds(q, GROUP, stride=BLOCK), :]
+        stores[half].start()
+    for half in range(2):
+        stores[half].wait()
+
+
+def finish(w):
     return pl.pallas_call(
         finish_kernel,
-        grid=(4,),
         out_shape=jax.ShapeDtypeStruct((BLOCK, GROUP, NR), f32),
-        in_specs=[
-            pl.BlockSpec((NR, NR), lambda n: (0, 0)),
-            pl.BlockSpec((2, GROUP, GROUP, HALF), lambda n: (0, 0, n, 0)),
+        in_specs=[pl.BlockSpec(memory_space=pltpu.HBM)],
+        out_specs=pl.BlockSpec(memory_space=pltpu.HBM),
+        scratch_shapes=[
+            pltpu.VMEM((2, NPHI, HALF), f32),
+            pltpu.VMEM((2, BLOCK, GROUP, HALF), f32),
+            pltpu.SemaphoreType.DMA((2,)),
+            pltpu.SemaphoreType.DMA((2,)),
         ],
-        out_specs=pl.BlockSpec((GROUP, GROUP, NR), lambda n: (n, 0, 0)),
-        scratch_shapes=[pltpu.VMEM((2, GROUP * GROUP, HALF), f32)],
-        compiler_params=pltpu.CompilerParams(vmem_limit_bytes=16 << 20),
+        compiler_params=pltpu.CompilerParams(vmem_limit_bytes=63 << 20),
         name="finish",
-    )(perm, w)
+    )(w)
 
 
 def body(tables, charge, outer_held, end_held):
-    forward, backward, *hartleys = (jnp.asarray(t) for t in tables)
-    outer = outer_held.reshape(1, NZ)
-    end = end_held.reshape(1, NR)
-    w, scales = run(charge, outer, end, (forward, *hartleys))
-    potential = finish(backward, w.reshape(2, GROUP, BLOCK, HALF))
-    return (potential, scales)
+    hartleys = tuple(jnp.asarray(t) for t in tables)
+    flat = charge.reshape(BLOCK * GROUP, NR)
+    w, scales = run(flat, outer_held.reshape(1, NZ), end_held.reshape(1, NR), hartleys)
+    return (finish(w), scales)
 
 
 def solution(mesh):
     in_specs = (P("phi", "gz", None), P(), P())
     out_specs = (P("phi", "gz", None), P(None, "phi"))
-    perm = parity_table()
-    tables = (perm, np.ascontiguousarray(perm.T), *hartley_tables())
     return jax.shard_map(
-        functools.partial(body, tables), mesh=mesh, in_specs=in_specs, out_specs=out_specs, check_vma=False
+        functools.partial(body, hartley_tables()),
+        mesh=mesh,
+        in_specs=in_specs,
+        out_specs=out_specs,
+        check_vma=False,
     )

time: 118 us -> 113 us (0.958)
  Pallas kernels: 115 us -> 112 us
  local copies, waits for them, and re-layouts: 1.79 us -> 0.57 us
    pallas_call x1, Pallas kernels: 113 us -> 109 us  [run(): pl.pallas_call(main_kernel, out_shape=(jax.ShapeDtypeStruct((2, NPHI, HAL...]
    unnamed x7 -> x3, local copies, waits for them, and re-layouts: 1.79 us -> 0.57 us
where the time goes in v4:
time: 113 us
  Pallas kernels  112 us (99%)
    pallas_call x1, Pallas kernels, run(): pl.pallas_call(main_kernel, out_shape=(jax.ShapeDtypeStruct((2, NPHI, HAL...  109 us
    pallas_call x1, Pallas kernels, finish(): pl.pallas_call(finish_kernel, out_shape=jax.ShapeDtypeStruct((BLOCK, GROU...  2.49 us

profile of v4, /device:TPU:1, one launch (start us, length us, event | category | flops | bytes accessed | tf_op | source)
XLA Modules:
  0.0 112.9 jit_solution(3521971936519758545)
XLA Ops:
  0.6 109.2 %modes.1 = (f32[2,1024,128]{2,1,0:T(8,128)}, f32[2,64]{1,0:T(2,128)}) custom-call(f32[1024,256]{1,0:T(8,128)} %bitcast.3, s32[1,256]{1,0:T(1,128)} %bitcast.4, s32[1,256]{1,0:T(1,128)} %bitcast.5, bf16[1024,1024]{1,0:T(8,128)(2,1)} %constant.8.clone.fh_ref, bf16[1024,1024]{1,0:T(8,128)(2,1)} %constant.9.clone.fl_ref, ...), custom_call_target="tpu_custom_call" | custom-call | tf_op jit(solution)/shard_map/modes/pallas_call | solution.py:498
  109.8 0.0 copy-start
  109.8 2.5 %finish.1 = f32[64,16,256]{2,1,0:T(8,128)} custom-call(f32[2,1024,128]{2,1,0:T(8,128)} %get-tuple-element.4.w_ref), custom_call_target="tpu_custom_call" | custom-call | tf_op jit(solution)/shard_map/finish/pallas_call | solution.py:554
  112.3 0.0 copy-done
  112.3 0.6 copy.10
Async XLA Ops:
  109.8 2.5 %copy-start = (f32[2,64]{1,0:T(2,128)S(1)}, f32[2,64]{1,0:T(2,128)}, u32[]{:S(2)}) copy-start(f32[2,64]{1,0:T(2,128)} %get-tuple-element.9) | copy-start | bytes 1540

commit v5 on v4

--- a/solution.py
+++ b/solution.py
@@ -35,7 +35,7 @@
     k = np.arange(NPHI)
     phase = (np.outer(k, k) % NPHI) * (2.0 * math.pi / NPHI)
     table = ((np.cos(phase) + np.sin(phase)) / math.sqrt(NPHI)).astype(np.float32)
-    order = k.reshape(GROUP, GROUP, FEW).transpose(1, 2, 0).reshape(-1)
+    order = k.reshape(GROUP, GROUP, FEW).transpose(2, 1, 0).reshape(-1)
     table = table[order]
     high = table.astype(jnp.bfloat16)
     low = (table - high.astype(np.float32)).astype(jnp.bfloat16)
@@ -255,9 +255,9 @@
 
 
 class Exchange:
-    def __init__(self, axis, src, dst, send, recv, base):
+    def __init__(self, axis, src, dst, send, recv, base, by_mode=False):
         self.axis, self.src, self.dst, self.send, self.recv = axis, src, dst, send, recv
-        self.base = base
+        self.base, self.by_mode = base, by_mode
         self.me = lax.axis_index(axis)
 
     def copy(self, par, source, target, t, sem):
@@ -270,18 +270,24 @@
             device_id_type=MESH,
         )
 
+    def place(self, t, m):
+        if self.by_mode:
+            return pl.ds(pl.multiple_of(m * (GROUP * GROUP) + t * GROUP, GROUP), GROUP)
+        return pl.ds(pl.multiple_of(t * BLOCK + m * GROUP, GROUP), GROUP)
+
     def start(self, par, t):
         self.copy(par, block(t), block(self.me), t, par).start()
 
-    def start_all(self, par):
-        peers(self.me, lambda t: self.start(par, t))
-
     def start_mode(self, par, m, sem):
-        rows = lambda n: pl.ds(pl.multiple_of(n * BLOCK + m * GROUP, GROUP), GROUP)
-        peers(self.me, lambda t: self.copy(par, rows(t), rows(self.me), t, sem).start())
+        peers(
+            self.me,
+            lambda t: self.copy(par, self.place(t, m), self.place(self.me, m), t, sem).start(),
+        )
 
     def keep(self, par):
-        self.dst[par, block(self.me), :] = self.src[par, block(self.me), :]
+        for m in range(FEW):
+            here = self.place(self.me, m)
+            self.dst[par, here, :] = self.src[par, here, :]
 
     def whole(self, par, rows, sem):
         t = lax.rem(self.me + 1, GROUP)
@@ -297,27 +303,19 @@
         self.whole(par, (GROUP - 1) * BLOCK, par).wait_send()
 
 
-def hartley(high, low, src, par, order, xs, exchange):
+def hartley(high, low, src, dst, par, order, xs, first, ready):
     for piece in range(4):
         rows = pl.ds(piece * 256, 256)
         h, l = split(src[par, rows, :])
         xs[rows, :HALF] = jnp.dot(h, order, preferred_element_type=f32).astype(bf16)
         xs[rows, HALF:] = jnp.dot(l, order, preferred_element_type=f32).astype(bf16)
-    me = exchange.me
-
     def step(n, carry):
-        piece = lax.rem(me // 4 + n, 4)
+        piece = lax.rem(first + n, 4)
         rows = pl.ds(pl.multiple_of(piece * 256, 256), 256)
         both = jnp.dot(high[rows, :], xs[...], preferred_element_type=f32)
         rest = jnp.dot(low[rows, :], xs[:, :HALF], preferred_element_type=f32)
-        exchange.src[par, rows, :] = both[:, :HALF] + (both[:, HALF:] + rest)
-        for j in range(4):
-            t = piece * 4 + lax.rem(me + j, 4)
-
-            @pl.when(t != me)
-            def _():
-                exchange.start(par, t)
-
+        dst[par, rows, :] = both[:, :HALF] + (both[:, HALF:] + rest)
+        ready(piece)
         return carry
 
     lax.fori_loop(0, 4, step, 0)
@@ -352,11 +350,11 @@
         )
 
     first = Exchange("phi", t1, r1, send.at[0], recv, 0)
-    second = Exchange("gz", s1, r2, send.at[1], recv, 2)
-    third = Exchange("phi", r3, r4, send.at[2], recv, 4)
-    fourth = Exchange("phi", o4, p3, send.at[3], recv, 9)
-    fifth = Exchange("gz", p2, q1, send.at[4], recv, 17)
-    sixth = Exchange("phi", v1, w_ref, send.at[5], recv, 19)
+    second = Exchange("gz", s1, r2, send.at[1], recv, 2, True)
+    third = Exchange("phi", r3, r4, send.at[2], recv, 10)
+    fourth = Exchange("phi", o4, p3, send.at[3], recv, 15)
+    fifth = Exchange("gz", p2, q1, send.at[4], recv, 23, True)
+    sixth = Exchange("phi", v1, w_ref, send.at[5], recv, 25)
 
     for half in range(2):
         loads[half].wait()
@@ -396,19 +394,22 @@
 
     for par in range(2):
         first.wait_recv(par)
-        hartley(fh, fl, r1, par, order[par], xs, second)
+        hartley(
+            fh, fl, r1, s1, par, order[par], xs, 0,
+            lambda m: second.start_mode(par, m, par * FEW + m),
+        )
         second.keep(par)
-        second.wait_recv(par)
-        for b in range(GROUP):
-            for m in range(FEW):
+
+        def forward(m, carry):
+            second.wait_recv_mode(par, par * FEW + m)
+            for b in range(GROUP):
                 r3[par, pl.ds(m * GROUP + b, GROUP, stride=BLOCK), :] = r2[
-                    par, b * BLOCK + m * GROUP : b * BLOCK + (m + 1) * GROUP, :
+                    par, pl.ds(pl.multiple_of(m * (GROUP * GROUP) + b * GROUP, GROUP), GROUP), :
                 ]
-        if par == 0:
-            third.start_all(par)
-        else:
-            for m in range(FEW):
-                third.start_mode(par, m, 1 + m)
+            third.start_mode(par, m, par * (1 + m))
+            return carry
+
+        lax.fori_loop(0, FEW, forward, 0)
         third.keep(par)
 
     third.wait_recv(0)
@@ -459,17 +460,31 @@
     peers(gz, lambda t: scale_copy(sc_src, sc.at[gz], t).start())
     sc[gz] = sc_src[...]
 
+    def send_quarter(par, piece):
+        for n in range(4):
+            t = piece * 4 + lax.rem(phi + n, 4)
+
+            @pl.when(t != phi)
+            def _():
+                sixth.start(par, t)
+
     for par in range(2):
-        for m in range(FEW):
+
+        def backward(m, carry):
             fourth.wait_recv_mode(par, par * FEW + m)
             for b in range(GROUP):
-                p2[par, b * BLOCK + m * GROUP : b * BLOCK + (m + 1) * GROUP, :] = p3[
+                p2[par, pl.ds(pl.multiple_of(m * (GROUP * GROUP) + b * GROUP, GROUP), GROUP), :] = p3[
                     par, pl.ds(m * GROUP + b, GROUP, stride=BLOCK), :
                 ]
             fifth.start_mode(par, m, par)
+            return carry
+
+        lax.fori_loop(0, FEW, backward, 0)
         fifth.keep(par)
         fifth.wait_recv(par)
-        hartley(bh, bl, q1, par, order[2 + par], xs, sixth)
+        hartley(
+            bh, bl, q1, v1, par, order[2 + par], xs, phi // 4, lambda piece: send_quarter(par, piece)
+        )
         sixth.keep(par)
 
     others = sc.at[pl.ds(0, GROUP - 1)]
@@ -522,7 +537,7 @@
             pltpu.SemaphoreType.DMA((2,)),
             pltpu.SemaphoreType.DMA((6,)),
             pltpu.SemaphoreType.DMA((6, 2)),
-            pltpu.SemaphoreType.DMA((21,)),
+            pltpu.SemaphoreType.DMA((27,)),
             pltpu.SemaphoreType.DMA,
             pltpu.SemaphoreType.DMA,
         ],

time: 113 us -> 109 us (0.965)
  Pallas kernels: 112 us -> 108 us
    pallas_call x1, Pallas kernels: 109 us -> 105 us  [run(): pl.pallas_call(main_kernel, out_shape=(jax.ShapeDtypeStruct((2, NPHI, HAL...]
where the time goes in v5:
time: 109 us
  Pallas kernels  108 us (99%)
    pallas_call x1, Pallas kernels, run(): pl.pallas_call(main_kernel, out_shape=(jax.ShapeDtypeStruct((2, NPHI, HAL...  105 us
    pallas_call x1, Pallas kernels, finish(): pl.pallas_call(finish_kernel, out_shape=jax.ShapeDtypeStruct((BLOCK, GROU...  2.49 us

profile of v5, /device:TPU:1, one launch (start us, length us, event | category | flops | bytes accessed | tf_op | source)
XLA Modules:
  0.0 109.2 jit_solution(15715253549585769912)
XLA Ops:
  0.6 105.5 %modes.1 = (f32[2,1024,128]{2,1,0:T(8,128)}, f32[2,64]{1,0:T(2,128)}) custom-call(f32[1024,256]{1,0:T(8,128)} %bitcast.3, s32[1,256]{1,0:T(1,128)} %bitcast.4, s32[1,256]{1,0:T(1,128)} %bitcast.5, bf16[1024,1024]{1,0:T(8,128)(2,1)} %constant.8.clone.fh_ref, bf16[1024,1024]{1,0:T(8,128)(2,1)} %constant.9.clone.fl_ref, ...), custom_call_target="tpu_custom_call" | custom-call | tf_op jit(solution)/shard_map/modes/pallas_call | solution.py:513
  106.1 0.0 copy-start
  106.1 2.5 %finish.1 = f32[64,16,256]{2,1,0:T(8,128)} custom-call(f32[2,1024,128]{2,1,0:T(8,128)} %get-tuple-element.4.w_ref), custom_call_target="tpu_custom_call" | custom-call | tf_op jit(solution)/shard_map/finish/pallas_call | solution.py:569
  108.6 0.0 copy-done
  108.6 0.6 copy.10
Async XLA Ops:
  106.1 2.5 %copy-start = (f32[2,64]{1,0:T(2,128)S(1)}, f32[2,64]{1,0:T(2,128)}, u32[]{:S(2)}) copy-start(f32[2,64]{1,0:T(2,128)} %get-tuple-element.9) | copy-start | bytes 1540

commit v6 on v5

--- a/solution.py
+++ b/solution.py
@@ -245,6 +245,15 @@
     return pl.ds(pl.multiple_of(index * BLOCK, BLOCK), BLOCK)
 
 
+def far_peers(me, action):
+    def step(n, carry):
+        away = (GROUP // 2 - (n + 1) // 2) * (1 - 2 * lax.rem(n, 2))
+        action(lax.rem(me + GROUP + away, GROUP))
+        return carry
+
+    lax.fori_loop(0, GROUP - 1, step, 0)
+
+
 def peers(me, action):
     def step(n, carry):
         away = (n // 2 + 1) * (1 - 2 * lax.rem(n, 2))
@@ -324,24 +333,22 @@
 def main_kernel(
     charge_ref, outer_ref, end_ref, fh_ref, fl_ref, bh_ref, bl_ref,
     w_ref, s_ref,
-    outer, end, xin, t1, r1, s1, r2, r3, r4, o4, p3, p2, q1, v1, order, xs,
+    outer, end, r1, s1, r2, r3, r4, o4, p3, p2, q1, v1, order, xs,
     fh, fl, bh, bl,
     f, base, d, w, va, vb, r, ca, cb, cr, sc_src, sc,
-    in_sem, table_sem, send, recv, sc_send, sc_recv,
+    in_sem, table_sem, keep_sem, send, recv, sc_send, sc_recv,
 ):
     phi, gz = lax.axis_index("phi"), lax.axis_index("gz")
-    loads = [
-        pltpu.make_async_copy(charge_ref.at[:, pl.ds(half * HALF, HALF)], xin.at[half], in_sem.at[half])
+    own_loads = [
+        pltpu.make_async_copy(
+            charge_ref.at[:, phi, pl.ds(half * HALF, HALF)], r1.at[half, block(phi)], in_sem.at[half]
+        )
         for half in range(2)
     ]
-    for copy in loads:
-        copy.start()
     tables = [
         pltpu.make_async_copy(src, dst, table_sem.at[n])
         for n, (src, dst) in enumerate(((outer_ref, outer), (end_ref, end), (fh_ref, fh), (fl_ref, fl), (bh_ref, bh), (bl_ref, bl)))
     ]
-    for copy in tables:
-        copy.start()
     barrier = pltpu.get_barrier_semaphore()
     for axis, me in (("phi", phi), ("gz", gz)):
         peers(
@@ -349,24 +356,30 @@
             lambda t: pl.semaphore_signal(barrier, inc=1, device_id={axis: t}, device_id_type=MESH),
         )
 
-    first = Exchange("phi", t1, r1, send.at[0], recv, 0)
+    first = Exchange("phi", s1, r1, send.at[0], recv, 0)
     second = Exchange("gz", s1, r2, send.at[1], recv, 2, True)
     third = Exchange("phi", r3, r4, send.at[2], recv, 10)
     fourth = Exchange("phi", o4, p3, send.at[3], recv, 15)
     fifth = Exchange("gz", p2, q1, send.at[4], recv, 23, True)
-    sixth = Exchange("phi", v1, w_ref, send.at[5], recv, 25)
+    sixth = Exchange("phi", v1, q1, send.at[5], recv, 25)
+
+    pl.semaphore_wait(barrier, 2 * (GROUP - 1))
+
+    def first_copy(half, t):
+        return pltpu.make_async_remote_copy(
+            src_ref=charge_ref.at[:, t, pl.ds(half * HALF, HALF)],
+            dst_ref=r1.at[half, block(phi)],
+            send_sem=send.at[0, half],
+            recv_sem=recv.at[half],
+            device_id={"phi": t},
+            device_id_type=MESH,
+        )
 
     for half in range(2):
-        loads[half].wait()
-        if half == 0:
-            pl.semaphore_wait(barrier, 2 * (GROUP - 1))
-
-        def regroup(t):
-            t1[half, block(t), :] = xin[half, pl.ds(t, BLOCK, stride=GROUP), :]
-            first.start(half, t)
-
-        peers(phi, regroup)
-        r1[half, block(phi), :] = xin[half, pl.ds(phi, BLOCK, stride=GROUP), :]
+        far_peers(phi, lambda t: first_copy(half, t).start())
+        own_loads[half].start()
+    for copy in tables:
+        copy.start()
 
     for copy in tables:
         copy.wait()
@@ -394,6 +407,7 @@
 
     for par in range(2):
         first.wait_recv(par)
+        own_loads[par].wait()
         hartley(
             fh, fl, r1, s1, par, order[par], xs, 0,
             lambda m: second.start_mode(par, m, par * FEW + m),
@@ -460,13 +474,28 @@
     peers(gz, lambda t: scale_copy(sc_src, sc.at[gz], t).start())
     sc[gz] = sc_src[...]
 
+    def last_copy(par, t):
+        return pltpu.make_async_remote_copy(
+            src_ref=v1.at[par, block(t)],
+            dst_ref=w_ref.at[:, phi, pl.ds(par * HALF, HALF)],
+            send_sem=send.at[5, par],
+            recv_sem=recv.at[25 + par],
+            device_id={"phi": t},
+            device_id_type=MESH,
+        )
+
+    def own_copy(par):
+        return pltpu.make_async_copy(
+            v1.at[par, block(phi)], w_ref.at[:, phi, pl.ds(par * HALF, HALF)], keep_sem.at[par]
+        )
+
     def send_quarter(par, piece):
         for n in range(4):
             t = piece * 4 + lax.rem(phi + n, 4)
 
             @pl.when(t != phi)
             def _():
-                sixth.start(par, t)
+                last_copy(par, t).start()
 
     for par in range(2):
 
@@ -485,7 +514,7 @@
         hartley(
             bh, bl, q1, v1, par, order[2 + par], xs, phi // 4, lambda piece: send_quarter(par, piece)
         )
-        sixth.keep(par)
+        own_copy(par).start()
 
     others = sc.at[pl.ds(0, GROUP - 1)]
     all_scales = scale_copy(others, others, lax.rem(gz + 1, GROUP))
@@ -502,6 +531,7 @@
     for par in range(2):
         sixth.wait_recv(par)
         sixth.wait_send(par)
+        own_copy(par).wait()
 
 
 def run(charge, outer, end, tables):
@@ -513,15 +543,15 @@
     return pl.pallas_call(
         main_kernel,
         out_shape=(
-            jax.ShapeDtypeStruct((2, NPHI, HALF), f32),
+            jax.ShapeDtypeStruct((BLOCK, GROUP, NR), f32),
             jax.ShapeDtypeStruct((VCYC, BLOCK), f32),
         ),
         in_specs=[away] * 7,
-        out_specs=(whole, whole),
+        out_specs=(away, whole),
         scratch_shapes=[
             pltpu.VMEM((1, NZ), jnp.int32),
             pltpu.VMEM((1, NR), jnp.int32),
-            *[rows() for _ in range(12)],
+            *[rows() for _ in range(10)],
             pltpu.VMEM((4, HALF, HALF), bf16),
             pltpu.VMEM((NPHI, NR), bf16),
             table(), table(), table(), table(),
@@ -536,6 +566,7 @@
             pltpu.VMEM((GROUP, 8, HALF), f32),
             pltpu.SemaphoreType.DMA((2,)),
             pltpu.SemaphoreType.DMA((6,)),
+            pltpu.SemaphoreType.DMA((2,)),
             pltpu.SemaphoreType.DMA((6, 2)),
             pltpu.SemaphoreType.DMA((27,)),
             pltpu.SemaphoreType.DMA,
@@ -548,45 +579,10 @@
     )(charge, outer, end, *tables)
 
 
-def finish_kernel(w_ref, o_ref, rows, out, load_sem, store_sem):
-    loads = [pltpu.make_async_copy(w_ref.at[half], rows.at[half], load_sem.at[half]) for half in range(2)]
-    stores = [
-        pltpu.make_async_copy(out.at[half], o_ref.at[:, :, pl.ds(half * HALF, HALF)], store_sem.at[half])
-        for half in range(2)
-    ]
-    for half in range(2):
-        loads[half].start()
-    for half in range(2):
-        loads[half].wait()
-        for q in range(BLOCK):
-            out[half, q] = rows[half, pl.ds(q, GROUP, stride=BLOCK), :]
-        stores[half].start()
-    for half in range(2):
-        stores[half].wait()
-
-
-def finish(w):
-    return pl.pallas_call(
-        finish_kernel,
-        out_shape=jax.ShapeDtypeStruct((BLOCK, GROUP, NR), f32),
-        in_specs=[pl.BlockSpec(memory_space=pltpu.HBM)],
-        out_specs=pl.BlockSpec(memory_space=pltpu.HBM),
-        scratch_shapes=[
-            pltpu.VMEM((2, NPHI, HALF), f32),
-            pltpu.VMEM((2, BLOCK, GROUP, HALF), f32),
-            pltpu.SemaphoreType.DMA((2,)),
-            pltpu.SemaphoreType.DMA((2,)),
-        ],
-        compiler_params=pltpu.CompilerParams(vmem_limit_bytes=63 << 20),
-        name="finish",
-    )(w)
-
-
 def body(tables, charge, outer_held, end_held):
     hartleys = tuple(jnp.asarray(t) for t in tables)
-    flat = charge.reshape(BLOCK * GROUP, NR)
-    w, scales = run(flat, outer_held.reshape(1, NZ), end_held.reshape(1, NR), hartleys)
-    return (finish(w), scales)
+    w, scales = run(charge, outer_held.reshape(1, NZ), end_held.reshape(1, NR), hartleys)
+    return (w, scales)
 
 
 def solution(mesh):

time: 109 us -> 108 us (level)
  Pallas kernels: 108 us -> 105 us
  local copies, waits for them, and re-layouts: 0.57 us -> 2.83 us
    pallas_call x2 -> x1, Pallas kernels: 108 us -> 105 us  [run(): pl.pallas_call(main_kernel, out_shape=(jax.ShapeDtypeStruct((BLOCK, GROUP...]
    unnamed x3 -> x4, local copies, waits for them, and re-layouts: 0.57 us -> 2.83 us
where the time goes in v6:
time: 108 us
  Pallas kernels  105 us (97%)
  local copies, waits for them, and re-layouts  2.83 us (3%)
    pallas_call x1, Pallas kernels, run(): pl.pallas_call(main_kernel, out_shape=(jax.ShapeDtypeStruct((BLOCK, GROUP...  105 us
    unnamed x4, local copies, waits for them, and re-layouts  2.83 us

profile of v6, /device:TPU:1, one launch (start us, length us, event | category | flops | bytes accessed | tf_op | source)
XLA Modules:
  0.0 108.2 jit_solution(18153423585781044660)
XLA Ops:
  0.6 104.7 %modes.1 = (f32[64,16,256]{2,1,0:T(8,128)}, f32[2,64]{1,0:T(2,128)}) custom-call(f32[64,16,256]{2,1,0:T(8,128)} %charge_ref.1, s32[1,256]{1,0:T(1,128)} %bitcast.2, s32[1,256]{1,0:T(1,128)} %bitcast.3, bf16[1024,1024]{1,0:T(8,128)(2,1)} %constant.8.clone.fh_ref, bf16[1024,1024]{1,0:T(8,128)(2,1)} %constant.9.clone.fl_ref, ...), custom_call_target="tpu_custom_call" | custom-call | tf_op jit(solution)/shard_map/modes/pallas_call | solution.py:543
  105.3 0.0 copy-start
  105.3 2.3 %copy.11 = f32[64,16,256]{2,1,0:T(8,128)} copy(f32[64,16,256]{2,1,0:T(8,128)} %get-tuple-element.4) | data formatting | bytes 2097152
  107.6 0.0 copy-done
  107.6 0.6 copy.12
Async XLA Ops:
  105.3 2.3 %copy-start = (f32[2,64]{1,0:T(2,128)S(1)}, f32[2,64]{1,0:T(2,128)}, u32[]{:S(2)}) copy-start(f32[2,64]{1,0:T(2,128)} %get-tuple-element.5) | copy-start | bytes 1540

commit v7 on v6

--- a/solution.py
+++ b/solution.py
@@ -273,7 +273,7 @@
         return pltpu.make_async_remote_copy(
             src_ref=self.src.at[par, source],
             dst_ref=self.dst.at[par, target],
-            send_sem=self.send.at[par],
+            send_sem=self.send,
             recv_sem=self.recv.at[self.base + sem],
             device_id={self.axis: t},
             device_id_type=MESH,
@@ -308,8 +308,9 @@
     def wait_recv_mode(self, par, sem):
         self.whole(par, (GROUP - 1) * GROUP, sem).wait_recv()
 
-    def wait_send(self, par):
-        self.whole(par, (GROUP - 1) * BLOCK, par).wait_send()
+    def wait_send(self):
+        rows = pl.ds(0, (GROUP - 1) * BLOCK)
+        self.copy(slice(None), rows, rows, lax.rem(self.me + 1, GROUP), 0).wait_send()
 
 
 def hartley(high, low, src, dst, par, order, xs, first, ready):
@@ -369,7 +370,7 @@
         return pltpu.make_async_remote_copy(
             src_ref=charge_ref.at[:, t, pl.ds(half * HALF, HALF)],
             dst_ref=r1.at[half, block(phi)],
-            send_sem=send.at[0, half],
+            send_sem=send.at[0],
             recv_sem=recv.at[half],
             device_id={"phi": t},
             device_id_type=MESH,
@@ -478,7 +479,7 @@
         return pltpu.make_async_remote_copy(
             src_ref=v1.at[par, block(t)],
             dst_ref=w_ref.at[:, phi, pl.ds(par * HALF, HALF)],
-            send_sem=send.at[5, par],
+            send_sem=send.at[5],
             recv_sem=recv.at[25 + par],
             device_id={"phi": t},
             device_id_type=MESH,
@@ -525,13 +526,12 @@
     s_ref[...] = total[:VCYC, :BLOCK]
 
     for exchange in (first, second, third, fourth, fifth):
-        for par in range(2):
-            exchange.wait_send(par)
+        exchange.wait_send()
     all_scales.wait_send()
     for par in range(2):
         sixth.wait_recv(par)
-        sixth.wait_send(par)
         own_copy(par).wait()
+    sixth.wait_send()
 
 
 def run(charge, outer, end, tables):
@@ -567,7 +567,7 @@
             pltpu.SemaphoreType.DMA((2,)),
             pltpu.SemaphoreType.DMA((6,)),
             pltpu.SemaphoreType.DMA((2,)),
-            pltpu.SemaphoreType.DMA((6, 2)),
+            pltpu.SemaphoreType.DMA((6,)),
             pltpu.SemaphoreType.DMA((27,)),
             pltpu.SemaphoreType.DMA,
             pltpu.SemaphoreType.DMA,
@@ -579,10 +579,41 @@
     )(charge, outer, end, *tables)
 
 
+def finish_kernel(w_ref, o_ref, held, load_sem, store_sem):
+    loads, stores = [], []
+    for n in range(4):
+        rows = pl.ds(GROUP * n, GROUP)
+        loads.append(pltpu.make_async_copy(w_ref.at[rows], held.at[rows], load_sem.at[n]))
+        stores.append(pltpu.make_async_copy(held.at[rows], o_ref.at[rows], store_sem.at[n]))
+    for copy in loads:
+        copy.start()
+    for load, store in zip(loads, stores):
+        load.wait()
+        store.start()
+    for copy in stores:
+        copy.wait()
+
+
+def finish(w):
+    return pl.pallas_call(
+        finish_kernel,
+        out_shape=jax.ShapeDtypeStruct((BLOCK, GROUP, NR), f32),
+        in_specs=[pl.BlockSpec(memory_space=pltpu.HBM)],
+        out_specs=pl.BlockSpec(memory_space=pltpu.HBM),
+        scratch_shapes=[
+            pltpu.VMEM((BLOCK, GROUP, NR), f32),
+            pltpu.SemaphoreType.DMA((4,)),
+            pltpu.SemaphoreType.DMA((4,)),
+        ],
+        compiler_params=pltpu.CompilerParams(vmem_limit_bytes=63 << 20),
+        name="finish",
+    )(w)
+
+
 def body(tables, charge, outer_held, end_held):
     hartleys = tuple(jnp.asarray(t) for t in tables)
     w, scales = run(charge, outer_held.reshape(1, NZ), end_held.reshape(1, NR), hartleys)
-    return (w, scales)
+    return (finish(w), scales)
 
 
 def solution(mesh):

time: 108 us -> 108 us (level)
  local copies, waits for them, and re-layouts: 2.83 us -> 0.57 us
  Pallas kernels: 105 us -> 107 us
    unnamed x4 -> x3, local copies, waits for them, and re-layouts: 2.83 us -> 0.57 us
    pallas_call x0 -> x1, Pallas kernels: none -> 1.98 us  [finish(): pl.pallas_call(finish_kernel, out_shape=jax.ShapeDtypeStruct((BLOCK, GROU...]
where the time goes in v7:
time: 108 us
  Pallas kernels  107 us (99%)
    pallas_call x1, Pallas kernels, run(): pl.pallas_call(main_kernel, out_shape=(jax.ShapeDtypeStruct((BLOCK, GROUP...  105 us

profile of v7, /device:TPU:1, one launch (start us, length us, event | category | flops | bytes accessed | tf_op | source)
XLA Modules:
  0.0 107.8 jit_solution(4382779834595397292)
XLA Ops:
  0.6 104.6 %modes.1 = (f32[64,16,256]{2,1,0:T(8,128)}, f32[2,64]{1,0:T(2,128)}) custom-call(f32[64,16,256]{2,1,0:T(8,128)} %charge_ref.1, s32[1,256]{1,0:T(1,128)} %bitcast.2, s32[1,256]{1,0:T(1,128)} %bitcast.3, bf16[1024,1024]{1,0:T(8,128)(2,1)} %constant.8.clone.fh_ref, bf16[1024,1024]{1,0:T(8,128)(2,1)} %constant.9.clone.fl_ref, ...), custom_call_target="tpu_custom_call" | custom-call | tf_op jit(solution)/shard_map/modes/pallas_call | solution.py:543
  105.3 0.0 copy-start
  105.3 2.0 %finish.1 = f32[64,16,256]{2,1,0:T(8,128)} custom-call(f32[64,16,256]{2,1,0:T(8,128)} %get-tuple-element.4.w_ref), custom_call_target="tpu_custom_call" | custom-call | tf_op jit(solution)/shard_map/finish/pallas_call | solution.py:598
  107.3 0.0 copy-done
  107.3 0.6 copy.10
Async XLA Ops:
  105.3 2.0 %copy-start = (f32[2,64]{1,0:T(2,128)S(1)}, f32[2,64]{1,0:T(2,128)}, u32[]{:S(2)}) copy-start(f32[2,64]{1,0:T(2,128)} %get-tuple-element.9) | copy-start | bytes 1540
